TPU v7x, 32 devices: a whole 2x2x4 slice. The times are simulated.
32 devices in a mesh: crops: 2 (over y), rows: 4 (over x, core), cols: 4 (over z).
Axes of the slice: x: 2, y: 2, z: 4, core: 2. Of those that a mesh axis runs over, the one named last changes fastest.
Arguments:
- pair_maps: bfloat16 [2, 64, 1024, 1024], P('crops', None, 'rows', 'cols'), parts along dimension 0, may hold values from -6 to 6
- conv_a: bfloat16 [2, 3, 64, 192], replicated, may hold values from -0.25 to 0.25
- bias_a: float32 [2, 64], replicated, may hold values from -3 to 3
- conv_b: bfloat16 [2, 3, 64, 192], replicated, may hold values from -0.25 to 0.25
- bias_b: float32 [2, 64], replicated, may hold values from -3 to 3
- out_weight: bfloat16 [37, 64], replicated, may hold values from -3 to 3
- out_bias: float32 [37], replicated, may hold values from -4 to 4
Outputs:
- log_probs: float32 [2, 37, 1024, 1024], P('crops', None, ('rows', 'cols')), parts along dimension 0
There are 2 independent parts, one for each index of `crops`. A program takes and returns all parts, laid end to end along the dimension named above; an argument that names none is the same for every part. Nothing has to cross between parts.
All inputs are finite; a program needn't handle non-finite values.
Results may differ from a plain program's by a relative error of at most 0.0045.
Values may be sent and summed in bfloat16 or wider, within the bound.
No kernel may reach another device: no remote copies, remote signals or barrier semaphores. Data moves between devices by JAX's collectives and lax.ppermute only.
A program may use at most 192 MiB of HBM per device.

v0:
```python
import functools

import jax
import jax.numpy as jnp
from jax import lax
from jax.experimental.layout import Layout, with_layout_constraint
from jax.experimental import pallas as pl
from jax.experimental.pallas import tpu as pltpu
from jax.sharding import PartitionSpec as P


BLOCKS = 2
D1 = 4
D2 = 8
CHUNKS = 2

FAR = 1 << 20
ROWS = 4
LEAD = 16


def chain_kernel(cfg, info_ref, t_ref, f_ref, b_ref, e_ref, wa_ref, ba_ref, wb_ref, bb_ref, wo_ref, bo_ref, o_ref, buf, side, sems, X, I, bias, acc, xa, xb):
    H, W, C, whole = cfg
    R = ROWS
    S = W + e_ref.shape[2]
    halo = BLOCKS * (D1 + D2)
    NB = R * S
    T = 256
    BF, F32 = jnp.bfloat16, jnp.float32
    start = info_ref[4]

    def moved(source, a, b, length, q):
        return pltpu.make_async_copy(source.at[pl.ds(a, length)], buf.at[pl.ds(b, length)], sems.at[q])

    middle = moved(f_ref, start, halo, H, 0)
    middle.start()
    sides = pltpu.make_async_copy(e_ref.at[pl.ds(start, H + 2 * halo)], side, sems.at[3])
    sides.start()
    for q, edge_ref, outer, a, b in ((1, t_ref, start == 0, start - halo, 0), (2, b_ref, start + H == whole, start + H, H + halo)):

        @pl.when(outer)
        def _(q=q, edge_ref=edge_ref, b=b):
            moved(edge_ref, 0, b, halo, q).start()

        @pl.when(jnp.logical_not(outer))
        def _(q=q, a=a, b=b):
            moved(f_ref, a, b, halo, q).start()

    def at(row):
        return pl.multiple_of(128 + (row + halo + LEAD) * S, 128)

    for k in range(BLOCKS):
        bias[2 * k] = jnp.broadcast_to(ba_ref[k], (C, 128))
        bias[2 * k + 1] = jnp.broadcast_to(bb_ref[k], (C, 128))
    middle.wait()
    sides.wait()
    moved(t_ref, 0, 0, halo, 1).wait()
    moved(b_ref, 0, H + halo, halo, 2).wait()

    def fill(i, _):
        parts = []
        for q in range(R):
            e = side[i * R + q]
            parts += [e[:, :halo], buf[i * R + q], e[:, halo:]]
        X[:, pl.ds(at(i * R - halo), NB)] = jnp.concatenate(parts, axis=1)
        return 0

    lax.fori_loop(0, (H + 2 * halo) // R, fill, 0)
    lane = lax.broadcasted_iota(jnp.int32, (8, NB), 1)
    col = lane % S
    dead = ((col < halo) & (info_ref[2] > 0)) | ((col >= halo + W) & (info_ref[3] > 0))
    rl = jnp.where(dead, 4 * FAR, lane // S)
    first = jnp.where(info_ref[0] > 0, -start, -FAR)
    last = jnp.where(info_ref[1] > 0, whole - start, FAR)

    def masked(v, row, t):
        p = rl[:, t:t + T]
        m = (p >= first - row) & (p < last - row)
        return jnp.where(m[None], v.reshape(C // 8, 8, T), 0.0).reshape(C, T)

    def biased(v, i):
        b = bias[i]
        return v + jnp.concatenate([b] * (T // 128), axis=1)

    def conv(src, d, w_ref, k, spare, emit):
        n = d // R
        ring = 2 * n + 1
        odd = H // R % 2
        lo = -spare - odd * R
        total = (H + 2 * spare) // R + odd + 2 * n

        def slot(j):
            return pl.multiple_of(lax.rem(j, ring) * NB, 128)

        def shift(j, xs):
            x = src[:, pl.ds(pl.multiple_of(at(lo - d + j * R) - 128, 128), NB + 256)]
            xs[0:C, :] = pltpu.roll(x, d, 1)[:, 128:128 + NB]
            xs[C:2 * C, :] = pltpu.roll(x, NB + 256 - d, 1)[:, 128:128 + NB]

        def step(j, xs, nxt):
            shift(j + 1, nxt)
            row = lo - d + j * R
            s0, s1, s2 = slot(j), slot(j + ring - n), slot(j + ring - 2 * n)
            for t in range(0, NB, T):
                x = jnp.concatenate([xs[0:C, t:t + T], src[:, pl.ds(at(row) + t, T)], xs[C:2 * C, t:t + T]], axis=0)
                y = jnp.dot(w_ref[k], x, preferred_element_type=F32)
                done = acc[:, pl.ds(s2 + t, T)] + y[2 * C:]
                acc[:, pl.ds(s1 + t, T)] += y[C:2 * C]
                acc[:, pl.ds(s0 + t, T)] = y[:C]
                emit(row - d, t, done)

        shift(0, xa)

        def body(i, _):
            step(2 * i, xa, xb)
            step(2 * i + 1, xb, xa)
            return 0

        lax.fori_loop(0, total // 2, body, 0)

    def block(k, carry):
        edge = (BLOCKS - k) * (D1 + D2)

        def emit_a(row, t, v):
            v = biased(v, 2 * k)
            e = jnp.where(v > 0, v, jnp.exp(v) - 1.0)
            I[:, pl.ds(at(row) + t, T)] = masked(e, row, t).astype(BF)

        conv(X, D1, wa_ref, k, edge - D1, emit_a)

        def emit_b(row, t, v):
            v = biased(v, 2 * k + 1) + X[:, pl.ds(at(row) + t, T)].astype(F32)
            X[:, pl.ds(at(row) + t, T)] = masked(v, row, t).astype(BF)

        conv(I, D2, wb_ref, k, edge - D1 - D2, emit_b)
        return carry

    lax.fori_loop(0, BLOCKS, block, 0)
    bo = jnp.broadcast_to(bo_ref[...], (bo_ref.shape[0], W))

    def project(i, _):
        x = X[:, pl.ds(at(i * R), NB)]
        for q in range(R):
            g = jnp.dot(wo_ref[...], x[:, q * S + halo:q * S + halo + W], preferred_element_type=F32) + bo
            o_ref[i * R + q] = g.astype(BF)
        return 0

    lax.fori_loop(0, H // R, project, 0)


def chain(info, top, field, bottom, side, wa, ba, wb, bb, wo, bo, H):
    whole, C, W = field.shape
    S = W + side.shape[2]
    K = wo.shape[0]
    R = ROWS
    halo = BLOCKS * (D1 + D2)
    N = 128 + (H + 2 * halo + LEAD + R) * S + 256
    KP = -(-K // 16) * 16
    wo = jnp.pad(wo, ((0, KP - K), (0, 0)))
    bo = jnp.pad(bo, (0, KP - K))[:, None]
    vm = pl.BlockSpec(memory_space=pltpu.VMEM)
    ring = (2 * (max(D1, D2) // R) + 1) * R * S
    flops = 2 * BLOCKS * 2 * 9 * C * C * H * S
    out = pl.pallas_call(
        functools.partial(chain_kernel, (H, W, C, whole)),
        out_shape=jax.ShapeDtypeStruct((H, KP, W), jnp.bfloat16),
        in_specs=[pl.BlockSpec(memory_space=pltpu.SMEM), *[pl.BlockSpec(memory_space=pltpu.HBM)] * 4] + [vm] * 6,
        out_specs=vm,
        scratch_shapes=[
            pltpu.VMEM((H + 2 * halo, C, W), jnp.bfloat16),
            pltpu.VMEM((H + 2 * halo, C, S - W), jnp.bfloat16),
            pltpu.SemaphoreType.DMA((4,)),
            pltpu.VMEM((C, N), jnp.bfloat16),
            pltpu.VMEM((C, N), jnp.bfloat16),
            pltpu.VMEM((2 * BLOCKS, C, 128), jnp.float32),
            pltpu.VMEM((C, ring), jnp.float32),
            pltpu.VMEM((2 * C, R * S), jnp.bfloat16),
            pltpu.VMEM((2 * C, R * S), jnp.bfloat16),
        ],
        compiler_params=pltpu.CompilerParams(vmem_limit_bytes=63000 * 1024),
        cost_estimate=pl.CostEstimate(flops=flops, bytes_accessed=4 * C * H * S, transcendentals=2 * C * H * S),
        name="chain",
    )(info, top, field, bottom, side, wa, ba[:, :, None], wb, bb[:, :, None], wo, bo)
    return out[:, :K]


def neighbours(first, last, axis):
    peers = lax.axis_size(axis)
    up = [(i, i + 1) for i in range(peers - 1)]
    down = [(j, i) for i, j in up]
    return lax.ppermute(last, axis, up), lax.ppermute(first, axis, down)


def rims(tile):
    halo = BLOCKS * (D1 + D2)
    W = tile.shape[2]
    above, below = neighbours(tile[:, :halo], tile[:, -halo:], "rows")
    lane = jnp.arange(2 * halo)
    pick = jnp.where(lane < halo, lane, W - 2 * halo + lane)[:, None] == jnp.arange(W)[None, :]
    ends = jnp.einsum("dq,cpq->cdp", pick.astype(tile.dtype), tile, preferred_element_type=tile.dtype)
    left, right = neighbours(ends[:, :halo], ends[:, halo:], "cols")
    sides = jnp.concatenate([left, right], axis=1)
    up, down = neighbours(sides[:, :, :halo], sides[:, :, -halo:], "rows")
    corners = jnp.stack([up[:, :halo], up[:, halo:], down[:, :halo], down[:, halo:]], axis=1)
    return above, below, left, right, corners


def shards(pair_maps, conv_a, bias_a, conv_b, bias_b, out_weight, out_bias):
    rows, cols = lax.axis_size("rows"), lax.axis_size("cols")
    _, C, H, W = pair_maps.shape
    halo = BLOCKS * (D1 + D2)
    r, c = lax.axis_index("rows"), lax.axis_index("cols")
    edge = jnp.stack([r == 0, r == rows - 1, c == 0, c == cols - 1]).astype(jnp.int32)
    tile = pair_maps[0]
    above, below, left, right, corners = rims(tile)
    flat = jnp.concatenate

    def sides(left, right, corners, second, third):
        west = flat([corners[:, 0], left, corners[:, third]], axis=2)
        east = flat([corners[:, second], right, corners[:, 3]], axis=2)
        return west, east

    def caller(top, field, bottom, west, east, wa, wb, length):
        gap = jnp.zeros((C, 64 - 2 * halo, west.shape[2]), west.dtype)
        west, east, top, bottom = (with_layout_constraint(v, Layout((0, 1, 2))) for v in (west, east, top, bottom))
        side = with_layout_constraint(flat([west, east, gap], axis=1), Layout((0, 1, 2)))
        side, top, bottom = lax.optimization_barrier((side, top, bottom))
        side, top, bottom = jnp.transpose(side, (2, 0, 1)), jnp.transpose(top, (1, 0, 2)), jnp.transpose(bottom, (1, 0, 2))
        return lambda info: chain(info, top, field, bottom, side, wa, bias_a, wb, bias_b, out_weight, out_bias, length)

    square_grid = rows == 4 and cols == 4 and H == W and H // rows == 64

    def merged(w):
        return w.reshape(BLOCKS, 3 * C, 3 * C)

    if square_grid:
        me = r * cols + c
        homes = plan(cols)
        turn, off = (jnp.array([homes.get((i // cols, i % cols), (0, 0, 0))[q] for i in range(rows * cols)])[me] for q in (1, 2))
        field = lax.cond(turn > 0, lambda v: jnp.transpose(v, (2, 0, 1)), lambda v: jnp.transpose(v, (1, 0, 2)), tile)
        fixed = with_layout_constraint(jnp.swapaxes(corners, 2, 3), Layout((0, 1, 2, 3)))
        corners = jnp.where(turn > 0, fixed[:, jnp.array([0, 2, 1, 3])], with_layout_constraint(corners, Layout((0, 1, 2, 3))))
        north, south, west, east = (jnp.where(turn > 0, a, b) for a, b in ((left, above), (right, below), (above, left), (below, right)))
        west, east = sides(west, east, corners, 1, 2)
        edge = jnp.where(turn > 0, edge[jnp.array([2, 3, 0, 1])], edge)

        def turned(w):
            other = jnp.transpose(w.reshape(BLOCKS, 3, C, 3, C), (0, 3, 2, 1, 4))
            return jnp.where(turn > 0, merged(other), merged(w))

        wa, wb = turned(conv_a), turned(conv_b)
        q = cols // CHUNKS
        run = caller(north, field, south, west, east, wa, wb, H // CHUNKS)
        chunks, strips, recs = [], [], []
        for j in range(CHUNKS):
            info = jnp.append(edge, ((j * q) ^ (off & ~(q - 1))) * (H // cols))
            if j:
                info, *_ = lax.optimization_barrier((info, *strips[-q:]))
            chunks.append(jnp.transpose(run(info), (1, 0, 2)))
            for m in range(j * q, j * q + q):
                strips.append(lax.dynamic_slice_in_dim(chunks[j], ((m % q) ^ (off & (q - 1))) * (H // cols), H // cols, 1))
                perm = [(i * cols + k, home * cols + (m ^ o)) for (i, k), (home, _, o) in homes.items()]
                recs.append(lax.ppermute(strips[m], ("rows", "cols"), perm))
        return square(chunks, strips, recs)
    field = jnp.transpose(tile, (1, 0, 2))
    west, east = sides(left, right, corners, 1, 2)
    logits = caller(above, field, below, west, east, merged(conv_a), merged(conv_b), H)(jnp.append(edge, 0))
    logits = jnp.transpose(logits, (1, 0, 2))[None]
    strips = lax.all_to_all(logits, "cols", split_axis=2, concat_axis=3, tiled=True)
    flipped = lax.all_to_all(strips, ("rows", "cols"), split_axis=3, concat_axis=2, tiled=True)
    mirrored = jnp.swapaxes(flipped, 2, 3)
    symmetric = (strips.astype(jnp.float32) + mirrored.astype(jnp.float32)) * 0.5
    return symmetric - jnp.log(jnp.sum(jnp.exp(symmetric), axis=1, keepdims=True))


def pair_kernel(n, where_ref, r0, r1, r2, r3, o_ref, msg, lab, sems):
    K, sub, lanes = r0.shape
    r, s, keeps = where_ref[0], where_ref[1], where_ref[2]
    g = pl.program_id(0)
    W = lanes * pl.num_programs(0)

    def out(p, tile):
        spot = pl.multiple_of(lax.rem(tile, n) * W + g * lanes, lanes)
        return pltpu.make_async_copy(lab.at[p], o_ref.at[:, :, pl.ds(spot, lanes)], sems.at[p])

    for p, (one, two) in enumerate(((r0, r2), (r1, r3))):
        total = jnp.zeros((sub, lanes), jnp.float32)
        for k in range(K):
            v = (one[k].astype(jnp.float32) + two[k].astype(jnp.float32)) * 0.5
            lab[p, k] = v
            total = total + jnp.exp(v)
        norm = jnp.log(total)
        for k in range(K):
            v = lab[p, k] - norm
            lab[p, k] = v
            w = v.T
            for t in range(lanes // sub):
                b = w[t * sub:(t + 1) * sub]
                msg[p, t, k] = jnp.concatenate([b[:sub // 2], b[sub // 2:]], axis=1).astype(jnp.bfloat16)

        @pl.when(lax.rem(s, 2) == p)
        def _(p=p):
            out(p, r + 1).start()

        @pl.when((lax.rem(s, 2) != p) & (keeps > 0))
        def _(p=p):
            out(p, r + 2).start()

    for p in range(2):

        @pl.when((lax.rem(s, 2) == p) | (keeps > 0))
        def _(p=p):
            out(p, 0).wait()


def pairs(where, recs):
    K, sub, W = recs[0].shape
    lanes, n = 128, len(recs)
    return pl.pallas_call(
        functools.partial(pair_kernel, n),
        grid=(W // lanes,),
        in_specs=[pl.BlockSpec(memory_space=pltpu.SMEM)] + [pl.BlockSpec((K, sub, lanes), lambda i: (0, 0, i))] * 4,
        out_specs=[
            pl.BlockSpec(memory_space=pltpu.HBM),
            pl.BlockSpec((2, lanes // sub, K, sub // 2, 2 * sub), lambda i: (0, i, 0, 0, 0)),
        ],
        out_shape=[
            jax.ShapeDtypeStruct((K, sub, n * W), jnp.float32),
            jax.ShapeDtypeStruct((2, W // sub, K, sub // 2, 2 * sub), jnp.bfloat16),
        ],
        scratch_shapes=[pltpu.VMEM((2, K, sub, lanes), jnp.float32), pltpu.SemaphoreType.DMA((2,))],
        name="pairs",
    )(where, *recs)


def own_kernel(a_ref, b_ref, o_ref, tmp):
    K = a_ref.shape[0]

    def add(k, total):
        v = (a_ref[k].astype(jnp.float32) + b_ref[k].astype(jnp.float32).T) * 0.5
        tmp[k] = v
        return total + jnp.exp(v)

    norm = jnp.log(lax.fori_loop(0, K, add, jnp.zeros(tmp.shape[1:], jnp.float32), unroll=2))

    def emit(k, carry):
        o_ref[k] = (tmp[k] - norm).astype(jnp.bfloat16)
        return carry

    lax.fori_loop(0, K, emit, 0, unroll=2)


def own_pairs(tile):
    K, H, W = tile.shape
    B = 128
    return pl.pallas_call(
        own_kernel,
        grid=(H // B, W // B),
        in_specs=[pl.BlockSpec((K, B, B), lambda i, j: (0, i, j)), pl.BlockSpec((K, B, B), lambda i, j: (0, j, i))],
        out_specs=pl.BlockSpec((K, B, B), lambda i, j: (0, i, j)),
        out_shape=jax.ShapeDtypeStruct((K, H, W), jnp.bfloat16),
        scratch_shapes=[pltpu.VMEM((K, B, B), jnp.float32)],
        cost_estimate=pl.CostEstimate(flops=6 * K * H * W, bytes_accessed=6 * K * H * W, transcendentals=K * H * W),
        name="own",
    )(tile, tile)


def place_kernel(n, where_ref, diag, near, far, _, o_ref, own, one, two, sems):
    K, sub, W = diag.shape
    r, s, keeps = where_ref[0], where_ref[1], where_ref[2]

    def out(source, tile, q):
        spot = pl.multiple_of(lax.rem(tile, n) * W, W)
        return pltpu.make_async_copy(source, o_ref.at[:, :, pl.ds(spot, W)], sems.at[q])

    def spread(source, target):
        def body(k, carry):
            pieces = []
            for b in range(n):
                v = source[lax.rem(s + n - b, n), k].astype(jnp.float32)
                pieces.append(jnp.concatenate([v[:, :sub], v[:, sub:]], axis=0))
            target[k] = jnp.concatenate(pieces, axis=1)
            return carry

        lax.fori_loop(0, K, body, 0, unroll=4)

    def widen(k, carry):
        own[k] = diag[k].astype(jnp.float32)
        return carry

    lax.fori_loop(0, K, widen, 0, unroll=4)
    out(own, r, 0).start()
    spread(near, one)
    out(one, r + n - 1, 1).start()

    @pl.when(keeps == 0)
    def _():
        spread(far, two)
        out(two, r + 2, 2).start()
        out(two, r + 2, 2).wait()

    out(own, r, 0).wait()
    out(one, r + n - 1, 1).wait()


def place(where, diag, near, far, result):
    K, sub, W = diag.shape
    n = near.shape[0]
    vm = pl.BlockSpec(memory_space=pltpu.VMEM)
    hbm = pl.BlockSpec(memory_space=pltpu.HBM)
    return pl.pallas_call(
        functools.partial(place_kernel, n),
        in_specs=[pl.BlockSpec(memory_space=pltpu.SMEM), vm, vm, vm, hbm],
        out_specs=hbm,
        out_shape=jax.ShapeDtypeStruct((K, sub, n * W), jnp.float32),
        input_output_aliases={4: 0},
        scratch_shapes=[pltpu.VMEM((K, sub, W), jnp.float32)] * 3 + [pltpu.SemaphoreType.DMA((3,))],
        compiler_params=pltpu.CompilerParams(vmem_limit_bytes=40 * 1024 * 1024),
        name="place",
    )(where, diag, near, far, result)


def plan(n):
    homes = {}
    for r in range(n):
        for c in range(n):
            gap = (c - r) % n
            if gap == 1:
                homes[r, c] = (r, 0, 0)
            elif gap == 3:
                homes[r, c] = (c, 1, 2)
            elif gap == 2:
                owner = 0 if 0 in (r, c) else 3
                homes[r, c] = (owner, int(r != owner), 1 if r == owner else 3)
    return homes


def square(chunks, strips, recs):
    n = lax.axis_size("rows")
    axes = ("rows", "cols")
    r, s = lax.axis_index("rows"), lax.axis_index("cols")
    sub = strips[0].shape[1]
    tile, *_ = lax.optimization_barrier((jnp.concatenate(chunks, axis=1), *strips))
    own = own_pairs(tile)
    diag = None
    for k in range(n):
        strip = lax.dynamic_slice_in_dim(own, lax.rem(r + k, n) * sub, sub, 1)
        if k == 0:
            diag = jnp.where(s == r, strip, jnp.zeros_like(strip))
        else:
            diag = diag + lax.ppermute(strip, axes, [(i * n + i, i * n + (i + k) % n) for i in range(n)])
    keeps = jnp.where((r == 0) | (r == n - 1), 1, 0)
    where = jnp.stack([r, s, keeps]).astype(jnp.int32)
    result, msg = pairs(where, recs)
    near, far = [], []
    for k in range(n):
        t = lax.rem(s + k, n)
        for half, kept, moves in ((lax.rem(s, 2), near, [(i, (i + 1) % n) for i in range(n)]), (1 - lax.rem(s, 2), far, [(0, 2), (3, 1)])):
            payload = lax.dynamic_slice(msg, (half, t, 0, 0, 0), (1, 1) + msg.shape[2:])[0, 0]
            perm = [(i * n + j, o * n + (j + k) % n) for i, o in moves for j in range(n)]
            kept.append(lax.ppermute(payload, axes, perm))
    return place(where, diag, jnp.stack(near), jnp.stack(far), result)[None]


def solution(mesh):
    in_specs = (P("crops", None, "rows", "cols"), P(), P(), P(), P(), P(), P())
    out_specs = P("crops", None, ("rows", "cols"), None)

    body = jax.shard_map(shards, mesh=mesh, in_specs=in_specs, out_specs=out_specs, check_vma=False)

    def run(*args):
        with jax.sharding.use_abstract_mesh(mesh.abstract_mesh):
            return body(*args)

    return run
```

profile of v0, /device:TPU:1, one launch (start us, length us, event | category | flops | bytes accessed | tf_op | source)
XLA Modules:
  0.0 371.8 jit_solution(14513376669886642514)
XLA Ops:
  0.0 5.9 %convolution_bitcast_fusion = bf16[64,48,256]{2,1,0:T(8,128)(2,1)S(1)} fusion(s32[48]{0:T(128)S(1)} %compare_select_fusion, bf16[1,64,256,256]{3,2,1,0:T(8,128)(2,1)} %param.13), kind=kOutput, calls=%fused_computation.5 | convolution fusion | flops 402665472 | bytes 9961664 | tf_op jit(solution)/shard_map/dq,cpq->cdp/dot_general | solution.py:200
  6.9 4.9 %collective-permute-start = (bf16[64,24,256]{2,1,0:T(8,128)(2,1)}, bf16[64,24,256]{2,1,0:T(8,128)(2,1)}, u32[]{:S(2)}, u32[]{:S(2)}) collective-permute-start(bf16[64,24,256]{2,1,0:T(8,128)(2,1)} %get-tuple-element.54), channel_id=1, source_target_pairs={{0,1},{1,2},{2,3},{4,5},{5,6},{6,7},{8,9},{9,10},{10,11},{12,13},{... | collective-permute-start | bytes 2359304 | tf_op jit(solution)/shard_map/ppermute | solution.py:191
  11.8 2.4 fusion.4
  14.2 4.1 %collective-permute-start.4 = (bf16[64,24,256]{2,1,0:T(8,128)(2,1)}, bf16[64,24,256]{2,1,0:T(8,128)(2,1)}, u32[]{:S(2)}, u32[]{:S(2)}) collective-permute-start(bf16[64,24,256]{2,1,0:T(8,128)(2,1)} %get-tuple-element.26), channel_id=1, source_target_pairs={{0,4},{4,8},{8,12},{1,5},{5,9},{9,13},{2,6},{6,10},{10,14},{3,7},{... | collective-permute-start | bytes 2359304 | tf_op jit(solution)/shard_map/ppermute | solution.py:191
  18.3 1.3 collective-permute-start.1
  19.6 1.9 collective-permute-start.5
  25.8 1.7 bitcast_select_fusion.1
  27.5 2.8 broadcast_select_fusion.1
  30.4 9.0 %collective-permute-done.1 = bf16[64,24,256]{2,1,0:T(8,128)(2,1)S(1)} collective-permute-done((bf16[64,24,256]{2,1,0:T(8,128)(2,1)S(1)}, bf16[64,24,256]{2,1,0:T(8,128)(2,1)S(1)}, u32[]{:S(2)}, u32[]{:S(2)}) %collective-permute-start.1) | collective-permute-done | bytes 786464 | tf_op jit(solution)/shard_map/ppermute | solution.py:191
  39.3 2.6 broadcast_select_fusion
  43.0 2.3 collective-permute-start.3
  50.1 12.1 %conditional.1 = (bf16[256,64,256]{2,1,0:T(8,128)(2,1)}) conditional(s32[]{:T(128)} %convert_element_type.14, bf16[64,256,256]{2,1,0:T(8,128)(2,1)} %bitcast.101, (bf16[64,256,256]{2,1,0:T(8,128)(2,1)}) %tuple.48), branch_computations={%region_0.1_spmd, %region_1.2_spmd} | conditional | bytes 16777224 | solution.py:240
  50.1 12.1 %copy.78 = bf16[256,64,256]{2,1,0:T(8,128)(2,1)} copy(bf16[256,64,256]{0,2,1:T(8,128)(2,1)} %bitcast.104) | data formatting | bytes 16777216 | tf_op jit(solution)/shard_map/cond | solution.py:240
  63.6 3.4 collective-permute-start.2
  67.1 3.4 collective-permute-done.2
  71.6 2.2 copy.55
  73.8 2.3 gather_fusion.1
  77.7 2.4 maximum_maximum_fusion
  82.4 9.3 %copy.61 = bf16[64,64,304]{1,0,2:T(8,128)(2,1)} copy(bf16[64,64,304]{2,1,0:T(8,128)(2,1)S(1)} %maximum_maximum_fusion) | data formatting | bytes 4980736 | tf_op jit(solution)/shard_map/optimization_barrier | solution.py:227
  91.7 62.2 %chain.2 = bf16[128,48,256]{2,1,0:T(8,128)(2,1)} custom-call(s32[5]{0:T(128)} %get-tuple-element.61.info_ref, bf16[24,64,256]{2,1,0:T(8,128)(2,1)} %bitcast.112, bf16[256,64,256]{2,1,0:T(8,128)(2,1)} %get-tuple-element.24.f_ref, bf16[24,64,256]{2,1,0:T(8,128)(2,1)} %bitcast.114, bf16[304,64,64]{2,1,0:T(8,128)(2,1)} %bitcast.108, ...), custom_call_target="tpu_custom_call" | custom-call | flops 12079595520 | bytes 10485760 | tf_op jit(solution)/shard_map/chain/pallas_call | solution.py:164
  153.9 1.9 slice.82
  157.4 1.8 dynamic-slice_bitcast_fusion.2
  159.2 1.9 collective-permute-start.9
  161.1 2.5 collective-permute-start.10
  163.6 62.3 %chain.3 = bf16[128,48,256]{2,1,0:T(8,128)(2,1)} custom-call(s32[5]{0:T(128)} %get-tuple-element.20.info_ref, bf16[24,64,256]{2,1,0:T(8,128)(2,1)} %bitcast.113, bf16[256,64,256]{2,1,0:T(8,128)(2,1)} %get-tuple-element.24.f_ref, bf16[24,64,256]{2,1,0:T(8,128)(2,1)} %bitcast.115, bf16[304,64,64]{2,1,0:T(8,128)(2,1)} %bitcast.109, ...), custom_call_target="tpu_custom_call" | custom-call | flops 12079595520 | bytes 10485760 | tf_op jit(solution)/shard_map/chain/pallas_call | solution.py:164
  226.0 2.5 copy.89
  229.9 1.7 dynamic-slice_bitcast_fusion
  231.6 1.9 collective-permute-start.11
  233.5 9.7 %collective-permute-start.12 = (bf16[37,64,256]{2,1,0:T(8,128)(2,1)}, bf16[37,64,256]{2,1,0:T(8,128)(2,1)}, u32[]{:S(2)}, u32[]{:S(2)}) collective-permute-start(bf16[37,64,256]{2,1,0:T(8,128)(2,1)} %get-tuple-element.39), channel_id=1, source_target_pairs={{1,3},{2,2},{3,13},{4,1},{6,7},{7,12},{8,0},{9,5},{11,11},{12,15},... | collective-permute-start | bytes 3637256 | tf_op jit(solution)/shard_map/ppermute | solution.py:263
  243.2 2.5 pad_maximum_fusion.a_ref.b_ref
  245.7 12.6 %own.1 = bf16[37,256,256]{2,1,0:T(8,128)(2,1)} custom-call(bf16[37,256,256]{2,1,0:T(8,128)(2,1)} %pad_maximum_fusion.a_ref.b_ref, bf16[37,256,256]{2,1,0:T(8,128)(2,1)} %pad_maximum_fusion.a_ref.b_ref), custom_call_target="tpu_custom_call" | custom-call | flops 14548992 | bytes 14548992 | tf_op jit(solution)/shard_map/own/pallas_call | solution.py:356
  258.3 4.0 %constant_dynamic-slice_fusion.2 = (bf16[37,64,256]{2,1,0:T(8,128)(2,1)}, bf16[37,64,256]{2,1,0:T(8,128)(2,1)}, bf16[37,64,256]{2,1,0:T(8,128)(2,1)}) fusion(bf16[37,256,256]{2,1,0:T(8,128)(2,1)} %own.1, s32[]{:T(128)S(6)} %select_n.148, s32[]{:T(128)S(6)} %select_n.150, s32[]{:T(128)S(6)} %select_n.149), kind=kLoop, calls=%fused_computation.47 | loop fusion | bytes 7274508 | tf_op jit(solution)/shard_map/dynamic_slice | solution.py:447
  262.4 1.5 collective-permute-start.8
  265.7 1.7 collective-permute-start.6
  268.0 6.0 %pairs.1 = (f32[37,64,1024]{2,1,0:T(8,128)}, bf16[2,4,37,32,128]{4,3,2,1,0:T(8,128)(2,1)}) custom-call(s32[3]{0:T(128)} %pad_add_fusion.where_ref, bf16[37,64,256]{2,1,0:T(8,128)(2,1)} %copy-done.7, bf16[37,64,256]{2,1,0:T(8,128)(2,1)} %collective-permute-done.10.r1, bf16[37,64,256]{2,1,0:T(8,128)(2,1)} %collective-permute-done.11.r2, ...), custom_call_target="tpu_custom_call" | custom-call | tf_op jit(solution)/shard_map/pairs/pallas_call | solution.py:319
  274.0 2.9 dynamic-slice_bitcast_fusion.7
  277.0 7.1 %collective-permute-start.16 = (bf16[37,32,128]{2,1,0:T(8,128)(2,1)}, bf16[37,32,128]{2,1,0:T(8,128)(2,1)}, u32[]{:S(2)}, u32[]{:S(2)}) collective-permute-start(bf16[37,32,128]{2,1,0:T(8,128)(2,1)} %get-tuple-element.35), channel_id=1, source_target_pairs={{0,7},{1,4},{2,5},{3,6},{4,11},{5,8},{6,9},{7,10},{8,15},{9,12},{1... | collective-permute-start | bytes 909320 | tf_op jit(solution)/shard_map/ppermute | solution.py:461
  284.0 14.1 %collective-permute-start.15 = (bf16[37,32,128]{2,1,0:T(8,128)(2,1)}, bf16[37,32,128]{2,1,0:T(8,128)(2,1)}, u32[]{:S(2)}, u32[]{:S(2)}) collective-permute-start(bf16[37,32,128]{2,1,0:T(8,128)(2,1)} %get-tuple-element.36), channel_id=1, source_target_pairs={{0,6},{1,7},{2,4},{3,5},{4,10},{5,11},{6,8},{7,9},{8,14},{9,15},{1... | collective-permute-start | bytes 909320 | tf_op jit(solution)/shard_map/ppermute | solution.py:461
  298.2 5.3 %collective-permute-start.14 = (bf16[37,32,128]{2,1,0:T(8,128)(2,1)}, bf16[37,32,128]{2,1,0:T(8,128)(2,1)}, u32[]{:S(2)}, u32[]{:S(2)}) collective-permute-start(bf16[37,32,128]{2,1,0:T(8,128)(2,1)} %get-tuple-element.37), channel_id=1, source_target_pairs={{0,5},{1,6},{2,7},{3,4},{4,9},{5,10},{6,11},{7,8},{8,13},{9,14},{1... | collective-permute-start | bytes 909320 | tf_op jit(solution)/shard_map/ppermute | solution.py:461
  303.5 22.3 %collective-permute-start.13 = (bf16[37,32,128]{2,1,0:T(8,128)(2,1)}, bf16[37,32,128]{2,1,0:T(8,128)(2,1)S(1)}, u32[]{:S(2)}, u32[]{:S(2)}) collective-permute-start(bf16[37,32,128]{2,1,0:T(8,128)(2,1)} %get-tuple-element.38), channel_id=1, source_target_pairs={{0,4},{1,5},{2,6},{3,7},{4,8},{5,9},{6,10},{7,11},{8,12},{9,13},{1... | collective-permute-start | bytes 909320 | tf_op jit(solution)/shard_map/ppermute | solution.py:461
  325.7 1.3 collective-permute-start.20
  327.0 1.3 collective-permute-start.19
  328.3 1.3 collective-permute-start.18
  329.6 9.1 %collective-permute-done.14 = bf16[37,32,128]{2,1,0:T(8,128)(2,1)} collective-permute-done((bf16[37,32,128]{2,1,0:T(8,128)(2,1)}, bf16[37,32,128]{2,1,0:T(8,128)(2,1)}, u32[]{:S(2)}, u32[]{:S(2)}) %collective-permute-start.14) | collective-permute-done | bytes 303136 | tf_op jit(solution)/shard_map/ppermute | solution.py:461
  340.0 2.5 add_add_fusion.diag
  342.5 1.3 pad_maximum_fusion.1.near
  344.6 20.3 %collective-permute-done.19 = bf16[37,32,128]{2,1,0:T(8,128)(2,1)S(1)} collective-permute-done((bf16[37,32,128]{2,1,0:T(8,128)(2,1)S(1)}, bf16[37,32,128]{2,1,0:T(8,128)(2,1)S(1)}, u32[]{:S(2)}, u32[]{:S(2)}) %collective-permute-start.19) | collective-permute-done | bytes 303136 | tf_op jit(solution)/shard_map/ppermute | solution.py:461
  366.2 5.4 %place.1 = f32[37,64,1024]{2,1,0:T(8,128)} custom-call(s32[3]{0:T(128)S(1)} %copy-done, bf16[37,64,256]{2,1,0:T(8,128)(2,1)S(1)} %add_add_fusion.diag, bf16[4,37,32,128]{3,2,1,0:T(8,128)(2,1)S(1)} %pad_maximum_fusion.1.near, bf16[4,37,32,128]{3,2,1,0:T(8,128)(2,1)S(1)} %pad_maximum_fusion.2.far, ...), custom_call_target="tpu_custom_call", output_to_operand_aliasing={{}: (4, {})} | custom-call | tf_op jit(solution)/shard_map/place/pallas_call | solution.py:411
  (94 shorter events, 24.0 us)
Async XLA Ops:
  6.9 20.6 %collective-permute-start = (bf16[64,24,256]{2,1,0:T(8,128)(2,1)}, bf16[64,24,256]{2,1,0:T(8,128)(2,1)}, u32[]{:S(2)}, u32[]{:S(2)}) collective-permute-start(bf16[64,24,256]{2,1,0:T(8,128)(2,1)} %get-tuple-element.54), channel_id=1, source_target_pairs={{0,1},{1,2},{2,3},{4,5},{5,6},{6,7},{8,9},{9,10},{10,11},{12,13},{... | collective-permute-start | bytes 2359304 | tf_op jit(solution)/shard_map/ppermute | solution.py:191
  11.8 9.7 %copy-start.8 = (bf16[2,3,64,192]{3,2,1,0:T(8,128)(2,1)S(1)}, bf16[2,3,64,192]{3,2,1,0:T(8,128)(2,1)}, u32[]{:S(2)}) copy-start(bf16[2,3,64,192]{3,2,1,0:T(8,128)(2,1)} %param.16) | copy-start | bytes 442372
  14.2 8.8 %copy-start.9 = (bf16[2,3,64,192]{3,2,1,0:T(8,128)(2,1)S(1)}, bf16[2,3,64,192]{3,2,1,0:T(8,128)(2,1)}, u32[]{:S(2)}) copy-start(bf16[2,3,64,192]{3,2,1,0:T(8,128)(2,1)} %param.14) | copy-start | bytes 442372
  14.2 13.3 %collective-permute-start.4 = (bf16[64,24,256]{2,1,0:T(8,128)(2,1)}, bf16[64,24,256]{2,1,0:T(8,128)(2,1)}, u32[]{:S(2)}, u32[]{:S(2)}) collective-permute-start(bf16[64,24,256]{2,1,0:T(8,128)(2,1)} %get-tuple-element.26), channel_id=1, source_target_pairs={{0,4},{4,8},{8,12},{1,5},{5,9},{9,13},{2,6},{6,10},{10,14},{3,7},{... | collective-permute-start | bytes 2359304 | tf_op jit(solution)/shard_map/ppermute | solution.py:191
  18.3 21.0 %collective-permute-start.1 = (bf16[64,24,256]{2,1,0:T(8,128)(2,1)S(1)}, bf16[64,24,256]{2,1,0:T(8,128)(2,1)S(1)}, u32[]{:S(2)}, u32[]{:S(2)}) collective-permute-start(bf16[64,24,256]{2,1,0:T(8,128)(2,1)S(1)} %get-tuple-element.53), channel_id=1, source_target_pairs={{1,0},{2,1},{3,2},{5,4},{6,5},{7,6},{9,8},{10,9},{11,10},{13,12},{... | collective-permute-start | bytes 2359304 | tf_op jit(solution)/shard_map/ppermute | solution.py:191
  19.6 19.7 %collective-permute-start.5 = (bf16[64,24,256]{2,1,0:T(8,128)(2,1)S(1)}, bf16[64,24,256]{2,1,0:T(8,128)(2,1)}, u32[]{:S(2)}, u32[]{:S(2)}) collective-permute-start(bf16[64,24,256]{2,1,0:T(8,128)(2,1)S(1)} %get-tuple-element.27), channel_id=1, source_target_pairs={{4,0},{8,4},{12,8},{5,1},{9,5},{13,9},{6,2},{10,6},{14,10},{7,3},{... | collective-permute-start | bytes 2359304 | tf_op jit(solution)/shard_map/ppermute | solution.py:191
  21.8 2.0 copy-start.13
  21.8 2.0 copy-start.14
  22.0 2.4 copy-start.17
  41.9 3.4 copy-start.15
  42.0 3.4 copy-start.16
  42.0 5.3 %copy-start.11 = (f32[2,64]{1,0:T(2,128)S(1)}, f32[2,64]{1,0:T(2,128)}, u32[]{:S(2)}) copy-start(f32[2,64]{1,0:T(2,128)} %param.15) | copy-start | bytes 1540
  42.0 6.0 %copy-start.12 = (f32[2,64]{1,0:T(2,128)S(1)}, f32[2,64]{1,0:T(2,128)}, u32[]{:S(2)}) copy-start(f32[2,64]{1,0:T(2,128)} %param.17) | copy-start | bytes 1540
  42.0 7.5 %copy-start.10 = (bf16[37,64]{1,0:T(8,128)(2,1)S(1)}, bf16[37,64]{1,0:T(8,128)(2,1)}, u32[]{:S(2)}) copy-start(bf16[37,64]{1,0:T(8,128)(2,1)} %param.18) | copy-start | bytes 14212
  43.0 24.0 %collective-permute-start.3 = (bf16[64,48,24]{0,2,1:T(8,128)(2,1)S(1)}, bf16[64,48,24]{0,2,1:T(8,128)(2,1)S(1)}, u32[]{:S(2)}, u32[]{:S(2)}) collective-permute-start(bf16[64,48,24]{0,2,1:T(8,128)(2,1)S(1)} %copy.54), channel_id=1, source_target_pairs={{4,0},{8,4},{12,8},{5,1},{9,5},{13,9},{6,2},{10,6},{14,10},{7,3},{... | collective-permute-start | bytes 442376 | tf_op jit(solution)/shard_map/ppermute | solution.py:191
  63.6 6.9 %collective-permute-start.2 = (bf16[64,48,24]{0,2,1:T(8,128)(2,1)S(1)}, bf16[64,48,24]{0,2,1:T(8,128)(2,1)S(1)}, u32[]{:S(2)}, u32[]{:S(2)}) collective-permute-start(bf16[64,48,24]{0,2,1:T(8,128)(2,1)S(1)} %copy.53), channel_id=1, source_target_pairs={{0,4},{4,8},{8,12},{1,5},{5,9},{9,13},{2,6},{6,10},{10,14},{3,7},{... | collective-permute-start | bytes 442376 | tf_op jit(solution)/shard_map/ppermute | solution.py:191
  76.3 1.1 copy-start.2
  76.3 1.4 copy-start.3
  77.7 2.4 copy-start.4
  80.1 1.2 copy-start.5
  155.8 1.5 copy-start.1
  159.2 104.7 %collective-permute-start.9 = (bf16[37,64,256]{2,1,0:T(8,128)(2,1)}, bf16[37,64,256]{2,1,0:T(8,128)(2,1)S(1)}, u32[]{:S(2)}, u32[]{:S(2)}) collective-permute-start(bf16[37,64,256]{2,1,0:T(8,128)(2,1)} %get-tuple-element.42), channel_id=1, source_target_pairs={{1,0},{2,1},{3,14},{4,2},{6,4},{7,15},{8,3},{9,6},{11,8},{12,12},{... | collective-permute-start | bytes 3637256 | tf_op jit(solution)/shard_map/ppermute | solution.py:263
  161.1 104.6 %collective-permute-start.10 = (bf16[37,64,256]{2,1,0:T(8,128)(2,1)}, bf16[37,64,256]{2,1,0:T(8,128)(2,1)}, u32[]{:S(2)}, u32[]{:S(2)}) collective-permute-start(bf16[37,64,256]{2,1,0:T(8,128)(2,1)} %get-tuple-element.41), channel_id=1, source_target_pairs={{1,1},{2,0},{3,15},{4,3},{6,5},{7,14},{8,2},{9,7},{11,9},{12,13},{... | collective-permute-start | bytes 3637256 | tf_op jit(solution)/shard_map/ppermute | solution.py:263
  226.0 2.7 copy-start.6
  231.6 36.4 %collective-permute-start.11 = (bf16[37,64,256]{2,1,0:T(8,128)(2,1)}, bf16[37,64,256]{2,1,0:T(8,128)(2,1)}, u32[]{:S(2)}, u32[]{:S(2)}) collective-permute-start(bf16[37,64,256]{2,1,0:T(8,128)(2,1)} %get-tuple-element.40), channel_id=1, source_target_pairs={{1,2},{2,3},{3,12},{4,0},{6,6},{7,13},{8,1},{9,4},{11,10},{12,14},... | collective-permute-start | bytes 3637256 | tf_op jit(solution)/shard_map/ppermute | solution.py:263
  233.5 34.5 %collective-permute-start.12 = (bf16[37,64,256]{2,1,0:T(8,128)(2,1)}, bf16[37,64,256]{2,1,0:T(8,128)(2,1)}, u32[]{:S(2)}, u32[]{:S(2)}) collective-permute-start(bf16[37,64,256]{2,1,0:T(8,128)(2,1)} %get-tuple-element.39), channel_id=1, source_target_pairs={{1,3},{2,2},{3,13},{4,1},{6,7},{7,12},{8,0},{9,5},{11,11},{12,15},... | collective-permute-start | bytes 3637256 | tf_op jit(solution)/shard_map/ppermute | solution.py:263
  262.4 35.8 %collective-permute-start.8 = (bf16[37,64,256]{2,1,0:T(8,128)(2,1)}, bf16[37,64,256]{2,1,0:T(8,128)(2,1)S(1)}, u32[]{:S(2)}, u32[]{:S(2)}) collective-permute-start(bf16[37,64,256]{2,1,0:T(8,128)(2,1)} %get-tuple-element.29), channel_id=1, source_target_pairs={{0,3},{5,4},{10,9},{15,14},{16,19},{21,20},{26,25},{31,30}} | collective-permute-start | bytes 3637256 | tf_op jit(solution)/shard_map/ppermute | solution.py:451
  263.9 1.1 copy-start.7
  265.0 38.5 %collective-permute-start.7 = (bf16[37,64,256]{2,1,0:T(8,128)(2,1)}, bf16[37,64,256]{2,1,0:T(8,128)(2,1)S(1)}, u32[]{:S(2)}, u32[]{:S(2)}) collective-permute-start(bf16[37,64,256]{2,1,0:T(8,128)(2,1)} %get-tuple-element.30), channel_id=1, source_target_pairs={{0,2},{5,7},{10,8},{15,13},{16,18},{21,23},{26,24},{31,29}} | collective-permute-start | bytes 3637256 | tf_op jit(solution)/shard_map/ppermute | solution.py:451
  265.7 60.0 %collective-permute-start.6 = (bf16[37,64,256]{2,1,0:T(8,128)(2,1)}, bf16[37,64,256]{2,1,0:T(8,128)(2,1)}, u32[]{:S(2)}, u32[]{:S(2)}) collective-permute-start(bf16[37,64,256]{2,1,0:T(8,128)(2,1)} %get-tuple-element.28), channel_id=1, source_target_pairs={{0,1},{5,6},{10,11},{15,12},{16,17},{21,22},{26,27},{31,28}} | collective-permute-start | bytes 3637256 | tf_op jit(solution)/shard_map/ppermute | solution.py:451
  277.0 50.1 %collective-permute-start.16 = (bf16[37,32,128]{2,1,0:T(8,128)(2,1)}, bf16[37,32,128]{2,1,0:T(8,128)(2,1)}, u32[]{:S(2)}, u32[]{:S(2)}) collective-permute-start(bf16[37,32,128]{2,1,0:T(8,128)(2,1)} %get-tuple-element.35), channel_id=1, source_target_pairs={{0,7},{1,4},{2,5},{3,6},{4,11},{5,8},{6,9},{7,10},{8,15},{9,12},{1... | collective-permute-start | bytes 909320 | tf_op jit(solution)/shard_map/ppermute | solution.py:461
  284.0 44.3 %collective-permute-start.15 = (bf16[37,32,128]{2,1,0:T(8,128)(2,1)}, bf16[37,32,128]{2,1,0:T(8,128)(2,1)}, u32[]{:S(2)}, u32[]{:S(2)}) collective-permute-start(bf16[37,32,128]{2,1,0:T(8,128)(2,1)} %get-tuple-element.36), channel_id=1, source_target_pairs={{0,6},{1,7},{2,4},{3,5},{4,10},{5,11},{6,8},{7,9},{8,14},{9,15},{1... | collective-permute-start | bytes 909320 | tf_op jit(solution)/shard_map/ppermute | solution.py:461
  298.2 40.6 %collective-permute-start.14 = (bf16[37,32,128]{2,1,0:T(8,128)(2,1)}, bf16[37,32,128]{2,1,0:T(8,128)(2,1)}, u32[]{:S(2)}, u32[]{:S(2)}) collective-permute-start(bf16[37,32,128]{2,1,0:T(8,128)(2,1)} %get-tuple-element.37), channel_id=1, source_target_pairs={{0,5},{1,6},{2,7},{3,4},{4,9},{5,10},{6,11},{7,8},{8,13},{9,14},{1... | collective-permute-start | bytes 909320 | tf_op jit(solution)/shard_map/ppermute | solution.py:461
  303.5 39.1 %collective-permute-start.13 = (bf16[37,32,128]{2,1,0:T(8,128)(2,1)}, bf16[37,32,128]{2,1,0:T(8,128)(2,1)S(1)}, u32[]{:S(2)}, u32[]{:S(2)}) collective-permute-start(bf16[37,32,128]{2,1,0:T(8,128)(2,1)} %get-tuple-element.38), channel_id=1, source_target_pairs={{0,4},{1,5},{2,6},{3,7},{4,8},{5,9},{6,10},{7,11},{8,12},{9,13},{1... | collective-permute-start | bytes 909320 | tf_op jit(solution)/shard_map/ppermute | solution.py:461
  325.7 18.8 %collective-permute-start.20 = (bf16[37,32,128]{2,1,0:T(8,128)(2,1)}, bf16[37,32,128]{2,1,0:T(8,128)(2,1)S(1)}, u32[]{:S(2)}, u32[]{:S(2)}) collective-permute-start(bf16[37,32,128]{2,1,0:T(8,128)(2,1)} %get-tuple-element.32), channel_id=1, source_target_pairs={{0,11},{1,8},{2,9},{3,10},{12,7},{13,4},{14,5},{15,6},{16,27},{17,... | collective-permute-start | bytes 909320 | tf_op jit(solution)/shard_map/ppermute | solution.py:461
  327.0 37.9 %collective-permute-start.19 = (bf16[37,32,128]{2,1,0:T(8,128)(2,1)S(1)}, bf16[37,32,128]{2,1,0:T(8,128)(2,1)S(1)}, u32[]{:S(2)}, u32[]{:S(2)}) collective-permute-start(bf16[37,32,128]{2,1,0:T(8,128)(2,1)S(1)} %get-tuple-element.33), channel_id=1, source_target_pairs={{0,10},{1,11},{2,8},{3,9},{12,6},{13,7},{14,4},{15,5},{16,26},{17,... | collective-permute-start | bytes 909320 | tf_op jit(solution)/shard_map/ppermute | solution.py:461
  328.3 36.6 %collective-permute-start.18 = (bf16[37,32,128]{2,1,0:T(8,128)(2,1)S(1)}, bf16[37,32,128]{2,1,0:T(8,128)(2,1)S(1)}, u32[]{:S(2)}, u32[]{:S(2)}) collective-permute-start(bf16[37,32,128]{2,1,0:T(8,128)(2,1)S(1)} %get-tuple-element.34), channel_id=1, source_target_pairs={{0,9},{1,10},{2,11},{3,8},{12,5},{13,6},{14,7},{15,4},{16,25},{17,... | collective-permute-start | bytes 909320 | tf_op jit(solution)/shard_map/ppermute | solution.py:461
  338.7 27.3 %collective-permute-start.17 = (bf16[37,32,128]{2,1,0:T(8,128)(2,1)S(1)}, bf16[37,32,128]{2,1,0:T(8,128)(2,1)S(1)}, u32[]{:S(2)}, u32[]{:S(2)}) collective-permute-start(bf16[37,32,128]{2,1,0:T(8,128)(2,1)S(1)} %get-tuple-element.31), channel_id=1, source_target_pairs={{0,8},{1,9},{2,10},{3,11},{12,4},{13,5},{14,6},{15,7},{16,24},{17,... | collective-permute-start | bytes 909320 | tf_op jit(solution)/shard_map/ppermute | solution.py:461
  343.8 22.3 %copy-start = (s32[3]{0:T(128)S(1)}, s32[3]{0:T(128)}, u32[]{:S(2)}) copy-start(s32[3]{0:T(128)} %pad_add_fusion.where_ref) | copy-start | bytes 40
where the time goes:
time: 373 us; the launch traced here: 372 us
  Pallas kernels  149 us (40%)
  starting transfers between devices  91.7 us (25%)
  local copies, waits for them, and re-layouts  61.3 us (16%)
  waiting for transfers between devices  43.7 us (12%)
  other arithmetic  17.8 us (5%)
  matrix products  5.93 us (2%)
    pallas_call x2, Pallas kernels, chain(): pl.pallas_call(functools.partial(chain_kernel, (H, W, C, whole)), out_sha...  125 us
    ppermute x8, starting transfers between devices, square(): kept.append(lax.ppermute(payload, axes, perm))  53.9 us
    ppermute x8, waiting for transfers between devices, square(): kept.append(lax.ppermute(payload, axes, perm))  31.2 us
    ppermute x6, starting transfers between devices, neighbours(): return (lax.ppermute(last, axis, up), lax.ppermute(first, axis, down))  17.9 us
    ppermute x4, starting transfers between devices, shards(): recs.append(lax.ppermute(strips[m], ('rows', 'cols'), perm))  16 us
    pallas_call x1, Pallas kernels, own_pairs(): pl.pallas_call(own_kernel, grid=(H // B, W // B), in_specs=[pl.BlockSpec(...  12.6 us
    ppermute x6, waiting for transfers between devices, neighbours(): return (lax.ppermute(last, axis, up), lax.ppermute(first, axis, down))  12.4 us
    cond x1, local copies, waits for them, and re-layouts, shards(): lax.cond(turn > 0, lambda v: jnp.transpose(v, (2, 0, 1)), lambda v: jnp.t...  12.1 us
  transfers between devices with their start and end apart: 21, of which 6 were waited for; matrix products, arithmetic and copies ran while one was open for 13% of the time, Pallas kernels for 22%

commit v1 on v0

--- a/solution.py
+++ b/solution.py
@@ -236,7 +236,7 @@
     if square_grid:
         me = r * cols + c
         homes = plan(cols)
-        turn, off = (jnp.array([homes.get((i // cols, i % cols), (0, 0, 0))[q] for i in range(rows * cols)])[me] for q in (1, 2))
+        turn, off = (jnp.array([homes.get((i // cols, i % cols), (0, 0, 2 * (2 * i < rows * cols)))[q] for i in range(rows * cols)])[me] for q in (1, 2))
         field = lax.cond(turn > 0, lambda v: jnp.transpose(v, (2, 0, 1)), lambda v: jnp.transpose(v, (1, 0, 2)), tile)
         fixed = with_layout_constraint(jnp.swapaxes(corners, 2, 3), Layout((0, 1, 2, 3)))
         corners = jnp.where(turn > 0, fixed[:, jnp.array([0, 2, 1, 3])], with_layout_constraint(corners, Layout((0, 1, 2, 3))))
@@ -255,13 +255,16 @@
         for j in range(CHUNKS):
             info = jnp.append(edge, ((j * q) ^ (off & ~(q - 1))) * (H // cols))
             if j:
-                info, *_ = lax.optimization_barrier((info, *strips[-q:]))
+                info, *_ = lax.optimization_barrier((info, *strips[-q:], ahead))
             chunks.append(jnp.transpose(run(info), (1, 0, 2)))
             for m in range(j * q, j * q + q):
                 strips.append(lax.dynamic_slice_in_dim(chunks[j], ((m % q) ^ (off & (q - 1))) * (H // cols), H // cols, 1))
                 perm = [(i * cols + k, home * cols + (m ^ o)) for (i, k), (home, _, o) in homes.items()]
                 recs.append(lax.ppermute(strips[m], ("rows", "cols"), perm))
-        return square(chunks, strips, recs)
+            if not j:
+                ahead = own_pairs(lax.dynamic_slice_in_dim(chunks[0], (off & 2) * (H // cols), W // CHUNKS, 2))
+                early = crossing(ahead)
+        return square(chunks, strips, recs, early, off)
     field = jnp.transpose(tile, (1, 0, 2))
     west, east = sides(left, right, corners, 1, 2)
     logits = caller(above, field, below, west, east, merged(conv_a), merged(conv_b), H)(jnp.append(edge, 0))
@@ -365,8 +368,9 @@
     )(tile, tile)
 
 
-def place_kernel(n, where_ref, diag, near, far, _, o_ref, own, one, two, sems):
-    K, sub, W = diag.shape
+def place_kernel(n, where_ref, mine, other, e0, e1, l0, l1, near, far, _, o_ref, own, one, two, sems):
+    K, sub, W = mine.shape
+    F32 = jnp.float32
     r, s, keeps = where_ref[0], where_ref[1], where_ref[2]
 
     def out(source, tile, q):
@@ -384,11 +388,34 @@
 
         lax.fori_loop(0, K, body, 0, unroll=4)
 
-    def widen(k, carry):
-        own[k] = diag[k].astype(jnp.float32)
-        return carry
-
-    lax.fori_loop(0, K, widen, 0, unroll=4)
+    def each(fn):
+        def body(k, carry):
+            own[k] = fn(k)
+            return carry
+
+        lax.fori_loop(0, K, body, 0, unroll=4)
+
+    def both(a, b, k):
+        return a[k].astype(F32) + b[k].astype(F32)
+
+    beside = r + 1 - 2 * lax.rem(r, 2)
+
+    @pl.when(s == r)
+    def _():
+        each(lambda k: mine[k].astype(F32))
+
+    @pl.when(s == beside)
+    def _():
+        each(lambda k: other[k].astype(F32))
+
+    @pl.when((s != r) & (s != beside) & (2 * r < n))
+    def _():
+        each(lambda k: jnp.concatenate([both(l0, l1, k), both(e0, e1, k)], axis=1))
+
+    @pl.when((s != r) & (s != beside) & (2 * r >= n))
+    def _():
+        each(lambda k: jnp.concatenate([both(e0, e1, k), both(l0, l1, k)], axis=1))
+
     out(own, r, 0).start()
     spread(near, one)
     out(one, r + n - 1, 1).start()
@@ -404,20 +431,20 @@
 
 
 def place(where, diag, near, far, result):
-    K, sub, W = diag.shape
+    K, sub, W = diag[0].shape
     n = near.shape[0]
     vm = pl.BlockSpec(memory_space=pltpu.VMEM)
     hbm = pl.BlockSpec(memory_space=pltpu.HBM)
     return pl.pallas_call(
         functools.partial(place_kernel, n),
-        in_specs=[pl.BlockSpec(memory_space=pltpu.SMEM), vm, vm, vm, hbm],
+        in_specs=[pl.BlockSpec(memory_space=pltpu.SMEM), *[vm] * (len(diag) + 2), hbm],
         out_specs=hbm,
         out_shape=jax.ShapeDtypeStruct((K, sub, n * W), jnp.float32),
-        input_output_aliases={4: 0},
+        input_output_aliases={len(diag) + 3: 0},
         scratch_shapes=[pltpu.VMEM((K, sub, W), jnp.float32)] * 3 + [pltpu.SemaphoreType.DMA((3,))],
         compiler_params=pltpu.CompilerParams(vmem_limit_bytes=40 * 1024 * 1024),
         name="place",
-    )(where, diag, near, far, result)
+    )(where, *diag, near, far, result)
 
 
 def plan(n):
@@ -435,20 +462,71 @@
     return homes
 
 
-def square(chunks, strips, recs):
+def crossing(block):
+    n = lax.axis_size("rows")
+    sub = block.shape[1] // (n // 2)
+    got = []
+    for e in range(n // 2):
+        perm = [(i * n + i, i * n + (n // 2 if 2 * i < n else 0) + e) for i in range(n)]
+        got.append(lax.ppermute(block[:, e * sub:(e + 1) * sub], ("rows", "cols"), perm))
+    return got
+
+
+def rest_kernel(h_ref, a_ref, b_ref, c_ref, near_ref, far_ref, tmp):
+    K = a_ref.shape[0]
+    first = pl.program_id(0) == 0
+
+    def add(k, total):
+        other = jnp.where(first, b_ref[k].astype(jnp.float32), c_ref[k].astype(jnp.float32))
+        v = (a_ref[k].astype(jnp.float32) + other.T) * 0.5
+        tmp[k] = v
+        return total + jnp.exp(v)
+
+    norm = jnp.log(lax.fori_loop(0, K, add, jnp.zeros(tmp.shape[1:], jnp.float32), unroll=2))
+
+    def emit(k, carry):
+        v = tmp[k] - norm
+        near_ref[k] = v.astype(jnp.bfloat16)
+        far_ref[k] = v.T.astype(jnp.bfloat16)
+        return carry
+
+    lax.fori_loop(0, K, emit, 0, unroll=2)
+
+
+def rest_pairs(half, far_rows, near_rows):
+    K, B, W = near_rows.shape
+    return pl.pallas_call(
+        rest_kernel,
+        grid_spec=pltpu.PrefetchScalarGridSpec(
+            num_scalar_prefetch=1,
+            grid=(2,),
+            in_specs=[
+                pl.BlockSpec((K, B, B), lambda g, h: (0, 0, (1 - h[0]) * (1 - g) + h[0] * g)),
+                pl.BlockSpec((K, B, B), lambda g, h: (0, 0, 1 - h[0])),
+                pl.BlockSpec((K, B, B), lambda g, h: (0, 0, 1 - h[0])),
+            ],
+            out_specs=[
+                pl.BlockSpec((K, B, B), lambda g, h: (0, 0, (1 - h[0]) * (1 - g) + h[0] * g)),
+                pl.BlockSpec((K, B, B), lambda g, h: (0, 0, 0)),
+            ],
+            scratch_shapes=[pltpu.VMEM((K, B, B), jnp.float32)],
+        ),
+        out_shape=[jax.ShapeDtypeStruct((K, B, W), jnp.bfloat16), jax.ShapeDtypeStruct((K, B, B), jnp.bfloat16)],
+        cost_estimate=pl.CostEstimate(flops=6 * K * B * W, bytes_accessed=6 * K * B * W, transcendentals=K * B * W),
+        name="rest",
+    )(half, near_rows, near_rows, far_rows)
+
+
+def square(chunks, strips, recs, early, off):
     n = lax.axis_size("rows")
     axes = ("rows", "cols")
     r, s = lax.axis_index("rows"), lax.axis_index("cols")
     sub = strips[0].shape[1]
-    tile, *_ = lax.optimization_barrier((jnp.concatenate(chunks, axis=1), *strips))
-    own = own_pairs(tile)
-    diag = None
-    for k in range(n):
-        strip = lax.dynamic_slice_in_dim(own, lax.rem(r + k, n) * sub, sub, 1)
-        if k == 0:
-            diag = jnp.where(s == r, strip, jnp.zeros_like(strip))
-        else:
-            diag = diag + lax.ppermute(strip, axes, [(i * n + i, i * n + (i + k) % n) for i in range(n)])
+    far_rows, near_rows, *_ = lax.optimization_barrier((*chunks, *strips))
+    near, far = rest_pairs((off // 2)[None].astype(jnp.int32), far_rows, near_rows)
+    late = crossing(far)
+    mine, other = (lax.dynamic_slice_in_dim(near, v * sub, sub, 1) for v in (r % 2, 1 - r % 2))
+    other = lax.ppermute(other, axes, [(i * n + i, i * n + (i ^ 1)) for i in range(n)])
     keeps = jnp.where((r == 0) | (r == n - 1), 1, 0)
     where = jnp.stack([r, s, keeps]).astype(jnp.int32)
     result, msg = pairs(where, recs)
@@ -459,7 +537,7 @@
             payload = lax.dynamic_slice(msg, (half, t, 0, 0, 0), (1, 1) + msg.shape[2:])[0, 0]
             perm = [(i * n + j, o * n + (j + k) % n) for i, o in moves for j in range(n)]
             kept.append(lax.ppermute(payload, axes, perm))
-    return place(where, diag, jnp.stack(near), jnp.stack(far), result)[None]
+    return place(where, [mine, other, *early, *late], jnp.stack(near), jnp.stack(far), result)[None]
 
 
 def solution(mesh):

time: 373 us -> 417 us (1.12)
  the two profiles are of different devices: /device:TPU:1 before, /device:TPU:2 now
where the time goes in v1:
time: 417 us; the launch traced here: 415 us
  Pallas kernels  153 us (37%)
  waiting for transfers between devices  111 us (27%)
  starting transfers between devices  64 us (15%)
  local copies, waits for them, and re-layouts  63.3 us (15%)
  other arithmetic  12.8 us (3%)
  matrix products  5.93 us (1%)
  between operations  5.47 us (1%)
    pallas_call x2, Pallas kernels, chain(): pl.pallas_call(functools.partial(chain_kernel, (H, W, C, whole)), out_sha...  125 us
    ppermute x4, waiting for transfers between devices, crossing(): lax.ppermute(block[:, e * sub:(e + 1) * sub], ('rows', 'cols'), perm)  52.3 us
    ppermute x8, starting transfers between devices, square(): kept.append(lax.ppermute(payload, axes, perm))  29.9 us
    ppermute x4, waiting for transfers between devices, shards(): recs.append(lax.ppermute(strips[m], ('rows', 'cols'), perm))  26.5 us
    ppermute x8, waiting for transfers between devices, square(): kept.append(lax.ppermute(payload, axes, perm))  19.3 us
    ppermute x6, starting transfers between devices, neighbours(): return (lax.ppermute(last, axis, up), lax.ppermute(first, axis, down))  17.8 us
    ppermute x6, waiting for transfers between devices, neighbours(): return (lax.ppermute(last, axis, up), lax.ppermute(first, axis, down))  12.4 us
    cond x1, local copies, waits for them, and re-layouts, shards(): lax.cond(turn > 0, lambda v: jnp.transpose(v, (2, 0, 1)), lambda v: jnp.t...  12.1 us
  transfers between devices with their start and end apart: 23, of which 9 were waited for; matrix products, arithmetic and copies ran while one was open for 10% of the time, Pallas kernels for 18%

profile of v1, /device:TPU:2, one launch (start us, length us, event | category | flops | bytes accessed | tf_op | source)
XLA Modules:
  0.0 415.3 jit_solution(3996315091434972529)
XLA Ops:
  0.0 5.9 %convolution_bitcast_fusion = bf16[64,48,256]{2,1,0:T(8,128)(2,1)S(1)} fusion(s32[48]{0:T(128)S(1)} %compare_select_fusion, bf16[1,64,256,256]{3,2,1,0:T(8,128)(2,1)} %param.13), kind=kOutput, calls=%fused_computation.4 | convolution fusion | flops 402665472 | bytes 9961664 | tf_op jit(solution)/shard_map/dq,cpq->cdp/dot_general | solution.py:200
  6.9 4.4 %collective-permute-start = (bf16[64,24,256]{2,1,0:T(8,128)(2,1)}, bf16[64,24,256]{2,1,0:T(8,128)(2,1)}, u32[]{:S(2)}, u32[]{:S(2)}) collective-permute-start(bf16[64,24,256]{2,1,0:T(8,128)(2,1)} %get-tuple-element.59), channel_id=1, source_target_pairs={{0,1},{1,2},{2,3},{4,5},{5,6},{6,7},{8,9},{9,10},{10,11},{12,13},{... | collective-permute-start | bytes 2359304 | tf_op jit(solution)/shard_map/ppermute | solution.py:191
  11.3 2.4 fusion.4
  13.7 2.0 collective-permute-start.4
  17.0 3.6 collective-permute-start.5
  24.9 1.7 bitcast_select_fusion.1
  27.5 2.8 broadcast_select_fusion.1
  30.3 5.7 %collective-permute-done.1 = bf16[64,24,256]{2,1,0:T(8,128)(2,1)S(1)} collective-permute-done((bf16[64,24,256]{2,1,0:T(8,128)(2,1)S(1)}, bf16[64,24,256]{2,1,0:T(8,128)(2,1)S(1)}, u32[]{:S(2)}, u32[]{:S(2)}) %collective-permute-start.1) | collective-permute-done | bytes 786464 | tf_op jit(solution)/shard_map/ppermute | solution.py:191
  36.0 2.6 broadcast_select_fusion
  39.7 4.4 %collective-permute-start.3 = (bf16[64,48,24]{0,2,1:T(8,128)(2,1)S(1)}, bf16[64,48,24]{0,2,1:T(8,128)(2,1)S(1)}, u32[]{:S(2)}, u32[]{:S(2)}) collective-permute-start(bf16[64,48,24]{0,2,1:T(8,128)(2,1)S(1)} %copy.54), channel_id=1, source_target_pairs={{4,0},{8,4},{12,8},{5,1},{9,5},{13,9},{6,2},{10,6},{14,10},{7,3},{... | collective-permute-start | bytes 442376 | tf_op jit(solution)/shard_map/ppermute | solution.py:191
  49.2 12.1 %conditional.1 = (bf16[256,64,256]{2,1,0:T(8,128)(2,1)}) conditional(s32[]{:T(128)} %convert_element_type.14, bf16[64,256,256]{2,1,0:T(8,128)(2,1)} %bitcast.105, (bf16[64,256,256]{2,1,0:T(8,128)(2,1)}) %tuple.49), branch_computations={%region_0.1_spmd, %region_1.2_spmd} | conditional | bytes 16777224 | solution.py:240
  49.2 12.1 %copy.78 = bf16[256,64,256]{2,1,0:T(8,128)(2,1)} copy(bf16[256,64,256]{0,2,1:T(8,128)(2,1)} %bitcast.108) | data formatting | bytes 16777216 | tf_op jit(solution)/shard_map/cond | solution.py:240
  62.6 2.1 collective-permute-start.2
  64.8 5.9 %collective-permute-done.2 = bf16[64,48,24]{0,2,1:T(8,128)(2,1)S(1)} collective-permute-done((bf16[64,48,24]{0,2,1:T(8,128)(2,1)S(1)}, bf16[64,48,24]{0,2,1:T(8,128)(2,1)S(1)}, u32[]{:S(2)}, u32[]{:S(2)}) %collective-permute-start.2) | collective-permute-done | bytes 147488 | tf_op jit(solution)/shard_map/ppermute | solution.py:191
  71.8 2.2 copy.55
  74.0 2.3 gather_fusion.1
  77.9 2.4 maximum_maximum_fusion
  82.6 9.3 %copy.61 = bf16[64,64,304]{1,0,2:T(8,128)(2,1)} copy(bf16[64,64,304]{2,1,0:T(8,128)(2,1)S(1)} %maximum_maximum_fusion) | data formatting | bytes 4980736 | tf_op jit(solution)/shard_map/optimization_barrier | solution.py:227
  91.9 62.3 %chain.2 = bf16[128,48,256]{2,1,0:T(8,128)(2,1)} custom-call(s32[5]{0:T(128)} %get-tuple-element.71.info_ref, bf16[24,64,256]{2,1,0:T(8,128)(2,1)} %bitcast.117, bf16[256,64,256]{2,1,0:T(8,128)(2,1)} %get-tuple-element.30.f_ref, bf16[24,64,256]{2,1,0:T(8,128)(2,1)} %bitcast.119, bf16[304,64,64]{2,1,0:T(8,128)(2,1)} %bitcast.113, ...), custom_call_target="tpu_custom_call" | custom-call | flops 12079595520 | bytes 10485760 | tf_op jit(solution)/shard_map/chain/pallas_call | solution.py:164
  154.1 1.9 slice.98
  157.6 1.3 dynamic-slice_bitcast_fusion.2.a_ref.b_ref
  158.9 5.2 %own.1 = bf16[37,128,128]{2,1,0:T(8,128)(2,1)} custom-call(bf16[37,128,128]{2,1,0:T(8,128)(2,1)} %dynamic-slice_bitcast_fusion.2.a_ref.b_ref, bf16[37,128,128]{2,1,0:T(8,128)(2,1)} %dynamic-slice_bitcast_fusion.2.a_ref.b_ref), custom_call_target="tpu_custom_call" | custom-call | flops 3637248 | bytes 3637248 | tf_op jit(solution)/shard_map/own/pallas_call | solution.py:359
  164.0 1.6 dynamic-slice_bitcast_fusion.3
  165.6 1.4 collective-permute-start.12
  167.0 1.9 collective-permute-start.11
  168.9 62.3 %chain.3 = bf16[128,48,256]{2,1,0:T(8,128)(2,1)} custom-call(s32[5]{0:T(128)} %get-tuple-element.23.info_ref, bf16[24,64,256]{2,1,0:T(8,128)(2,1)} %bitcast.118, bf16[256,64,256]{2,1,0:T(8,128)(2,1)} %get-tuple-element.30.f_ref, bf16[24,64,256]{2,1,0:T(8,128)(2,1)} %bitcast.120, bf16[304,64,64]{2,1,0:T(8,128)(2,1)} %bitcast.114, ...), custom_call_target="tpu_custom_call" | custom-call | flops 12079595520 | bytes 10485760 | tf_op jit(solution)/shard_map/chain/pallas_call | solution.py:164
  231.2 1.9 slice.99
  234.6 1.7 dynamic-slice_bitcast_fusion
  236.3 2.4 collective-permute-start.14
  238.6 5.8 %collective-permute-start.13 = (bf16[37,64,256]{2,1,0:T(8,128)(2,1)}, bf16[37,64,256]{2,1,0:T(8,128)(2,1)}, u32[]{:S(2)}, u32[]{:S(2)}) collective-permute-start(bf16[37,64,256]{2,1,0:T(8,128)(2,1)} %get-tuple-element.45), channel_id=1, source_target_pairs={{1,2},{2,3},{3,12},{4,0},{6,6},{7,13},{8,1},{9,4},{11,10},{12,14},... | collective-permute-start | bytes 3637256 | tf_op jit(solution)/shard_map/ppermute | solution.py:263
  245.1 19.5 %collective-permute-done.14.r3 = bf16[37,64,256]{2,1,0:T(8,128)(2,1)} collective-permute-done((bf16[37,64,256]{2,1,0:T(8,128)(2,1)}, bf16[37,64,256]{2,1,0:T(8,128)(2,1)}, u32[]{:S(2)}, u32[]{:S(2)}) %collective-permute-start.14) | collective-permute-done | bytes 1212448 | tf_op jit(solution)/shard_map/ppermute | solution.py:263
  264.6 7.0 %collective-permute-done.13.r2 = bf16[37,64,256]{2,1,0:T(8,128)(2,1)} collective-permute-done((bf16[37,64,256]{2,1,0:T(8,128)(2,1)}, bf16[37,64,256]{2,1,0:T(8,128)(2,1)}, u32[]{:S(2)}, u32[]{:S(2)}) %collective-permute-start.13) | collective-permute-done | bytes 1212448 | tf_op jit(solution)/shard_map/ppermute | solution.py:263
  271.6 6.0 %pairs.1 = (f32[37,64,1024]{2,1,0:T(8,128)}, bf16[2,4,37,32,128]{4,3,2,1,0:T(8,128)(2,1)}) custom-call(s32[3]{0:T(128)} %pad_add_fusion.where_ref, bf16[37,64,256]{2,1,0:T(8,128)(2,1)} %copy-done.11, bf16[37,64,256]{2,1,0:T(8,128)(2,1)} %copy-done.10, bf16[37,64,256]{2,1,0:T(8,128)(2,1)} %collective-permute-done.13.r2, ...), custom_call_target="tpu_custom_call" | custom-call | tf_op jit(solution)/shard_map/pairs/pallas_call | solution.py:322
  277.6 3.1 dynamic-slice_bitcast_fusion.8
  282.0 1.3 collective-permute-start.22
  283.3 1.3 collective-permute-start.21
  284.6 1.3 collective-permute-start.20
  288.2 2.0 copy.90
  290.4 2.0 copy.89
  292.4 12.0 %rest.1 = (bf16[37,128,256]{2,1,0:T(8,128)(2,1)}, bf16[37,128,128]{2,1,0:T(8,128)(2,1)}) custom-call(s32[1]{0:T(128)} %bitcast.6.h_ref, bf16[37,128,256]{2,1,0:T(8,128)(2,1)} %bitcast.109, bf16[37,128,256]{2,1,0:T(8,128)(2,1)} %bitcast.110, bf16[37,128,256]{2,1,0:T(8,128)(2,1)} %bitcast.111), custom_call_target="tpu_custom_call" | custom-call | flops 7274496 | bytes 7274496 | tf_op jit(solution)/shard_map/rest/pallas_call | solution.py:498
  304.5 2.0 constant_dynamic-slice_fusion
  307.4 24.0 %collective-permute-start.18 = (bf16[37,32,128]{2,1,0:T(8,128)(2,1)S(1)}, bf16[37,32,128]{2,1,0:T(8,128)(2,1)S(1)}, u32[]{:S(2)}, u32[]{:S(2)}) collective-permute-start(bf16[37,32,128]{2,1,0:T(8,128)(2,1)S(1)} %copy-done.15), channel_id=1, source_target_pairs={{0,7},{1,4},{2,5},{3,6},{4,11},{5,8},{6,9},{7,10},{8,15},{9,12},{1... | collective-permute-start | bytes 909320 | tf_op jit(solution)/shard_map/ppermute | solution.py:539
  332.4 6.6 %collective-permute-done.18 = bf16[37,32,128]{2,1,0:T(8,128)(2,1)S(1)} collective-permute-done((bf16[37,32,128]{2,1,0:T(8,128)(2,1)S(1)}, bf16[37,32,128]{2,1,0:T(8,128)(2,1)S(1)}, u32[]{:S(2)}, u32[]{:S(2)}) %collective-permute-start.18) | collective-permute-done | bytes 303136 | tf_op jit(solution)/shard_map/ppermute | solution.py:539
  339.7 12.7 %collective-permute-done.17 = bf16[37,32,128]{2,1,0:T(8,128)(2,1)S(1)} collective-permute-done((bf16[37,32,128]{2,1,0:T(8,128)(2,1)S(1)}, bf16[37,32,128]{2,1,0:T(8,128)(2,1)S(1)}, u32[]{:S(2)}, u32[]{:S(2)}) %collective-permute-start.17) | collective-permute-done | bytes 303136 | tf_op jit(solution)/shard_map/ppermute | solution.py:539
  355.7 1.4 pad_maximum_fusion.1.far
  357.3 39.4 %collective-permute-done.7.e0 = bf16[37,64,128]{2,1,0:T(8,128)(2,1)S(1)} collective-permute-done((bf16[37,64,128]{2,1,0:T(8,128)(2,1)S(1)}, bf16[37,64,128]{2,1,0:T(8,128)(2,1)S(1)}, u32[]{:S(2)}, u32[]{:S(2)}) %collective-permute-start.7) | collective-permute-done | bytes 606240 | tf_op jit(solution)/shard_map/ppermute | solution.py:471
  396.6 13.0 %collective-permute-done.9.l0 = bf16[37,64,128]{2,1,0:T(8,128)(2,1)S(1)} collective-permute-done((bf16[37,64,128]{2,1,0:T(8,128)(2,1)S(1)}, bf16[37,64,128]{2,1,0:T(8,128)(2,1)S(1)}, u32[]{:S(2)}, u32[]{:S(2)}) %collective-permute-start.9) | collective-permute-done | bytes 606240 | tf_op jit(solution)/shard_map/ppermute | solution.py:471
  409.6 5.5 %place.1 = f32[37,64,1024]{2,1,0:T(8,128)} custom-call(s32[3]{0:T(128)S(1)} %copy-done, bf16[37,64,256]{2,1,0:T(8,128)(2,1)S(1)} %get-tuple-element.43.mine, bf16[37,64,256]{2,1,0:T(8,128)(2,1)S(1)} %collective-permute-done.6.other, bf16[37,64,128]{2,1,0:T(8,128)(2,1)S(1)} %collective-permute-done.7.e0, ...), custom_call_target="tpu_custom_call", output_to_operand_aliasing={{}: (9, {})} | custom-call | tf_op jit(solution)/shard_map/place/pallas_call | solution.py:438
  (112 shorter events, 28.3 us)
Async XLA Ops:
  6.9 20.6 %collective-permute-start = (bf16[64,24,256]{2,1,0:T(8,128)(2,1)}, bf16[64,24,256]{2,1,0:T(8,128)(2,1)}, u32[]{:S(2)}, u32[]{:S(2)}) collective-permute-start(bf16[64,24,256]{2,1,0:T(8,128)(2,1)} %get-tuple-element.59), channel_id=1, source_target_pairs={{0,1},{1,2},{2,3},{4,5},{5,6},{6,7},{8,9},{9,10},{10,11},{12,13},{... | collective-permute-start | bytes 2359304 | tf_op jit(solution)/shard_map/ppermute | solution.py:191
  11.3 9.4 %copy-start.14 = (bf16[2,3,64,192]{3,2,1,0:T(8,128)(2,1)S(1)}, bf16[2,3,64,192]{3,2,1,0:T(8,128)(2,1)}, u32[]{:S(2)}) copy-start(bf16[2,3,64,192]{3,2,1,0:T(8,128)(2,1)} %param.14) | copy-start | bytes 442372
  13.7 8.5 %copy-start.13 = (bf16[2,3,64,192]{3,2,1,0:T(8,128)(2,1)S(1)}, bf16[2,3,64,192]{3,2,1,0:T(8,128)(2,1)}, u32[]{:S(2)}) copy-start(bf16[2,3,64,192]{3,2,1,0:T(8,128)(2,1)} %param.16) | copy-start | bytes 442372
  13.7 13.8 %collective-permute-start.4 = (bf16[64,24,256]{2,1,0:T(8,128)(2,1)}, bf16[64,24,256]{2,1,0:T(8,128)(2,1)}, u32[]{:S(2)}, u32[]{:S(2)}) collective-permute-start(bf16[64,24,256]{2,1,0:T(8,128)(2,1)} %get-tuple-element.32), channel_id=1, source_target_pairs={{0,4},{4,8},{8,12},{1,5},{5,9},{9,13},{2,6},{6,10},{10,14},{3,7},{... | collective-permute-start | bytes 2359304 | tf_op jit(solution)/shard_map/ppermute | solution.py:191
  15.7 20.3 %collective-permute-start.1 = (bf16[64,24,256]{2,1,0:T(8,128)(2,1)S(1)}, bf16[64,24,256]{2,1,0:T(8,128)(2,1)S(1)}, u32[]{:S(2)}, u32[]{:S(2)}) collective-permute-start(bf16[64,24,256]{2,1,0:T(8,128)(2,1)S(1)} %get-tuple-element.58), channel_id=1, source_target_pairs={{1,0},{2,1},{3,2},{5,4},{6,5},{7,6},{9,8},{10,9},{11,10},{13,12},{... | collective-permute-start | bytes 2359304 | tf_op jit(solution)/shard_map/ppermute | solution.py:191
  17.0 19.0 %collective-permute-start.5 = (bf16[64,24,256]{2,1,0:T(8,128)(2,1)S(1)}, bf16[64,24,256]{2,1,0:T(8,128)(2,1)}, u32[]{:S(2)}, u32[]{:S(2)}) collective-permute-start(bf16[64,24,256]{2,1,0:T(8,128)(2,1)S(1)} %get-tuple-element.33), channel_id=1, source_target_pairs={{4,0},{8,4},{12,8},{5,1},{9,5},{13,9},{6,2},{10,6},{14,10},{7,3},{... | collective-permute-start | bytes 2359304 | tf_op jit(solution)/shard_map/ppermute | solution.py:191
  20.9 1.9 copy-start.23
  20.9 3.3 copy-start.19
  20.9 3.2 copy-start.20
  38.6 5.5 %copy-start.21 = (f32[37]{0:T(128)S(1)}, f32[37]{0:T(128)}, u32[]{:S(2)}) copy-start(f32[37]{0:T(128)} %param.19) | copy-start | bytes 448
  38.6 5.5 %copy-start.22 = (s32[16]{0:T(128)S(1)}, s32[16]{0:T(128)}, u32[]{:S(2)}) copy-start(s32[16]{0:T(128)} %constant.82.clone) | copy-start | bytes 196
  38.6 8.4 %copy-start.17 = (f32[2,64]{1,0:T(2,128)S(1)}, f32[2,64]{1,0:T(2,128)}, u32[]{:S(2)}) copy-start(f32[2,64]{1,0:T(2,128)} %param.15) | copy-start | bytes 1540
  38.6 9.2 %copy-start.18 = (f32[2,64]{1,0:T(2,128)S(1)}, f32[2,64]{1,0:T(2,128)}, u32[]{:S(2)}) copy-start(f32[2,64]{1,0:T(2,128)} %param.17) | copy-start | bytes 1540
  38.7 9.9 %copy-start.16 = (bf16[37,64]{1,0:T(8,128)(2,1)S(1)}, bf16[37,64]{1,0:T(8,128)(2,1)}, u32[]{:S(2)}) copy-start(bf16[37,64]{1,0:T(8,128)(2,1)} %param.18) | copy-start | bytes 14212
  39.7 25.1 %collective-permute-start.3 = (bf16[64,48,24]{0,2,1:T(8,128)(2,1)S(1)}, bf16[64,48,24]{0,2,1:T(8,128)(2,1)S(1)}, u32[]{:S(2)}, u32[]{:S(2)}) collective-permute-start(bf16[64,48,24]{0,2,1:T(8,128)(2,1)S(1)} %copy.54), channel_id=1, source_target_pairs={{4,0},{8,4},{12,8},{5,1},{9,5},{13,9},{6,2},{10,6},{14,10},{7,3},{... | collective-permute-start | bytes 442376 | tf_op jit(solution)/shard_map/ppermute | solution.py:191
  62.6 8.0 %collective-permute-start.2 = (bf16[64,48,24]{0,2,1:T(8,128)(2,1)S(1)}, bf16[64,48,24]{0,2,1:T(8,128)(2,1)S(1)}, u32[]{:S(2)}, u32[]{:S(2)}) collective-permute-start(bf16[64,48,24]{0,2,1:T(8,128)(2,1)S(1)} %copy.53), channel_id=1, source_target_pairs={{0,4},{4,8},{8,12},{1,5},{5,9},{9,13},{2,6},{6,10},{10,14},{3,7},{... | collective-permute-start | bytes 442376 | tf_op jit(solution)/shard_map/ppermute | solution.py:191
  76.5 1.1 copy-start.6
  76.5 1.4 copy-start.7
  77.9 2.4 copy-start.8
  80.3 1.2 copy-start.9
  156.1 1.5 copy-start.1
  165.6 79.4 %collective-permute-start.12 = (bf16[37,64,256]{2,1,0:T(8,128)(2,1)}, bf16[37,64,256]{2,1,0:T(8,128)(2,1)S(1)}, u32[]{:S(2)}, u32[]{:S(2)}) collective-permute-start(bf16[37,64,256]{2,1,0:T(8,128)(2,1)} %get-tuple-element.46), channel_id=1, source_target_pairs={{1,1},{2,0},{3,15},{4,3},{6,5},{7,14},{8,2},{9,7},{11,9},{12,13},{... | collective-permute-start | bytes 3637256 | tf_op jit(solution)/shard_map/ppermute | solution.py:263
  167.0 78.1 %collective-permute-start.11 = (bf16[37,64,256]{2,1,0:T(8,128)(2,1)}, bf16[37,64,256]{2,1,0:T(8,128)(2,1)S(1)}, u32[]{:S(2)}, u32[]{:S(2)}) collective-permute-start(bf16[37,64,256]{2,1,0:T(8,128)(2,1)} %get-tuple-element.47), channel_id=1, source_target_pairs={{1,0},{2,1},{3,14},{4,2},{6,4},{7,15},{8,3},{9,6},{11,8},{12,12},{... | collective-permute-start | bytes 3637256 | tf_op jit(solution)/shard_map/ppermute | solution.py:263
  233.1 1.5 copy-start.3
  236.3 28.3 %collective-permute-start.14 = (bf16[37,64,256]{2,1,0:T(8,128)(2,1)}, bf16[37,64,256]{2,1,0:T(8,128)(2,1)}, u32[]{:S(2)}, u32[]{:S(2)}) collective-permute-start(bf16[37,64,256]{2,1,0:T(8,128)(2,1)} %get-tuple-element.44), channel_id=1, source_target_pairs={{1,3},{2,2},{3,13},{4,1},{6,7},{7,12},{8,0},{9,5},{11,11},{12,15},... | collective-permute-start | bytes 3637256 | tf_op jit(solution)/shard_map/ppermute | solution.py:263
  238.6 32.9 %collective-permute-start.13 = (bf16[37,64,256]{2,1,0:T(8,128)(2,1)}, bf16[37,64,256]{2,1,0:T(8,128)(2,1)}, u32[]{:S(2)}, u32[]{:S(2)}) collective-permute-start(bf16[37,64,256]{2,1,0:T(8,128)(2,1)} %get-tuple-element.45), channel_id=1, source_target_pairs={{1,2},{2,3},{3,12},{4,0},{6,6},{7,13},{8,1},{9,4},{11,10},{12,14},... | collective-permute-start | bytes 3637256 | tf_op jit(solution)/shard_map/ppermute | solution.py:263
  245.1 26.5 %copy-start.10 = (bf16[37,64,256]{2,1,0:T(8,128)(2,1)}, bf16[37,64,256]{2,1,0:T(8,128)(2,1)S(1)}, u32[]{:S(2)}) copy-start(bf16[37,64,256]{2,1,0:T(8,128)(2,1)S(1)} %collective-permute-done.12.r1) | copy-start | bytes 3637252
  245.1 26.5 %copy-start.11 = (bf16[37,64,256]{2,1,0:T(8,128)(2,1)}, bf16[37,64,256]{2,1,0:T(8,128)(2,1)S(1)}, u32[]{:S(2)}) copy-start(bf16[37,64,256]{2,1,0:T(8,128)(2,1)S(1)} %collective-permute-done.11.r0) | copy-start | bytes 3637252
  277.6 10.6 %copy-start.2 = (bf16[128,37,256]{2,1,0:T(8,128)(2,1)S(1)}, bf16[128,37,256]{2,1,0:T(8,128)(2,1)}, u32[]{:S(2)}) copy-start(bf16[128,37,256]{2,1,0:T(8,128)(2,1)} %copy-done.1) | copy-start | bytes 7274500
  280.7 26.7 %collective-permute-start.19 = (bf16[37,32,128]{2,1,0:T(8,128)(2,1)}, bf16[37,32,128]{2,1,0:T(8,128)(2,1)}, u32[]{:S(2)}, u32[]{:S(2)}) collective-permute-start(bf16[37,32,128]{2,1,0:T(8,128)(2,1)} %get-tuple-element.34), channel_id=1, source_target_pairs={{0,8},{1,9},{2,10},{3,11},{12,4},{13,5},{14,6},{15,7},{16,24},{17,... | collective-permute-start | bytes 909320 | tf_op jit(solution)/shard_map/ppermute | solution.py:539
  282.0 49.4 %collective-permute-start.22 = (bf16[37,32,128]{2,1,0:T(8,128)(2,1)}, bf16[37,32,128]{2,1,0:T(8,128)(2,1)}, u32[]{:S(2)}, u32[]{:S(2)}) collective-permute-start(bf16[37,32,128]{2,1,0:T(8,128)(2,1)} %get-tuple-element.35), channel_id=1, source_target_pairs={{0,11},{1,8},{2,9},{3,10},{12,7},{13,4},{14,5},{15,6},{16,27},{17,... | collective-permute-start | bytes 909320 | tf_op jit(solution)/shard_map/ppermute | solution.py:539
  283.3 48.1 %collective-permute-start.21 = (bf16[37,32,128]{2,1,0:T(8,128)(2,1)}, bf16[37,32,128]{2,1,0:T(8,128)(2,1)}, u32[]{:S(2)}, u32[]{:S(2)}) collective-permute-start(bf16[37,32,128]{2,1,0:T(8,128)(2,1)} %get-tuple-element.36), channel_id=1, source_target_pairs={{0,10},{1,11},{2,8},{3,9},{12,6},{13,7},{14,4},{15,5},{16,26},{17,... | collective-permute-start | bytes 909320 | tf_op jit(solution)/shard_map/ppermute | solution.py:539
  284.6 47.4 %collective-permute-start.20 = (bf16[37,32,128]{2,1,0:T(8,128)(2,1)}, bf16[37,32,128]{2,1,0:T(8,128)(2,1)}, u32[]{:S(2)}, u32[]{:S(2)}) collective-permute-start(bf16[37,32,128]{2,1,0:T(8,128)(2,1)} %get-tuple-element.37), channel_id=1, source_target_pairs={{0,9},{1,10},{2,11},{3,8},{12,5},{13,6},{14,7},{15,4},{16,25},{17,... | collective-permute-start | bytes 909320 | tf_op jit(solution)/shard_map/ppermute | solution.py:539
  288.2 2.2 copy-start.4
  304.4 2.9 copy-start.15
  304.4 27.7 %copy-start.5 = (bf16[37,128,128]{2,1,0:T(8,128)(2,1)S(1)}, bf16[37,128,128]{2,1,0:T(8,128)(2,1)}, u32[]{:S(2)}) copy-start(bf16[37,128,128]{2,1,0:T(8,128)(2,1)} %own.1) | copy-start | bytes 3637252
  306.5 25.8 %copy-start.12 = (bf16[37,128,128]{2,1,0:T(8,128)(2,1)S(1)}, bf16[37,128,128]{2,1,0:T(8,128)(2,1)}, u32[]{:S(2)}) copy-start(bf16[37,128,128]{2,1,0:T(8,128)(2,1)} %get-tuple-element.27) | copy-start | bytes 3637252
  306.5 103.2 %collective-permute-start.6 = (bf16[37,64,256]{2,1,0:T(8,128)(2,1)S(1)}, bf16[37,64,256]{2,1,0:T(8,128)(2,1)S(1)}, u32[]{:S(2)}, u32[]{:S(2)}) collective-permute-start(bf16[37,64,256]{2,1,0:T(8,128)(2,1)S(1)} %get-tuple-element.42), channel_id=1, source_target_pairs={{0,1},{5,4},{10,11},{15,14},{16,17},{21,20},{26,27},{31,30}} | collective-permute-start | bytes 3637256 | tf_op jit(solution)/shard_map/ppermute | solution.py:529
  307.4 31.6 %collective-permute-start.18 = (bf16[37,32,128]{2,1,0:T(8,128)(2,1)S(1)}, bf16[37,32,128]{2,1,0:T(8,128)(2,1)S(1)}, u32[]{:S(2)}, u32[]{:S(2)}) collective-permute-start(bf16[37,32,128]{2,1,0:T(8,128)(2,1)S(1)} %copy-done.15), channel_id=1, source_target_pairs={{0,7},{1,4},{2,5},{3,6},{4,11},{5,8},{6,9},{7,10},{8,15},{9,12},{1... | collective-permute-start | bytes 909320 | tf_op jit(solution)/shard_map/ppermute | solution.py:539
  331.4 21.0 %collective-permute-start.17 = (bf16[37,32,128]{2,1,0:T(8,128)(2,1)S(1)}, bf16[37,32,128]{2,1,0:T(8,128)(2,1)S(1)}, u32[]{:S(2)}, u32[]{:S(2)}) collective-permute-start(bf16[37,32,128]{2,1,0:T(8,128)(2,1)S(1)} %get-tuple-element.39), channel_id=1, source_target_pairs={{0,6},{1,7},{2,4},{3,5},{4,10},{5,11},{6,8},{7,9},{8,14},{9,15},{1... | collective-permute-start | bytes 909320 | tf_op jit(solution)/shard_map/ppermute | solution.py:539
  331.4 22.3 %collective-permute-start.16 = (bf16[37,32,128]{2,1,0:T(8,128)(2,1)S(1)}, bf16[37,32,128]{2,1,0:T(8,128)(2,1)S(1)}, u32[]{:S(2)}, u32[]{:S(2)}) collective-permute-start(bf16[37,32,128]{2,1,0:T(8,128)(2,1)S(1)} %get-tuple-element.40), channel_id=1, source_target_pairs={{0,5},{1,6},{2,7},{3,4},{4,9},{5,10},{6,11},{7,8},{8,13},{9,14},{1... | collective-permute-start | bytes 909320 | tf_op jit(solution)/shard_map/ppermute | solution.py:539
  332.0 22.4 %collective-permute-start.15 = (bf16[37,32,128]{2,1,0:T(8,128)(2,1)S(1)}, bf16[37,32,128]{2,1,0:T(8,128)(2,1)S(1)}, u32[]{:S(2)}, u32[]{:S(2)}) collective-permute-start(bf16[37,32,128]{2,1,0:T(8,128)(2,1)S(1)} %get-tuple-element.41), channel_id=1, source_target_pairs={{0,4},{1,5},{2,6},{3,7},{4,8},{5,9},{6,10},{7,11},{8,12},{9,13},{1... | collective-permute-start | bytes 909320 | tf_op jit(solution)/shard_map/ppermute | solution.py:539
  339.0 18.3 %collective-permute-start.8 = (bf16[37,64,128]{2,1,0:T(8,128)(2,1)S(1)}, bf16[37,64,128]{2,1,0:T(8,128)(2,1)S(1)}, u32[]{:S(2)}, u32[]{:S(2)}) collective-permute-start(bf16[37,64,128]{2,1,0:T(8,128)(2,1)S(1)} %get-tuple-element.62), channel_id=1, source_target_pairs={{0,3},{5,7},{10,9},{15,13},{16,19},{21,23},{26,25},{31,29}} | collective-permute-start | bytes 1818632 | tf_op jit(solution)/shard_map/ppermute | solution.py:471
  352.4 44.3 %collective-permute-start.7 = (bf16[37,64,128]{2,1,0:T(8,128)(2,1)S(1)}, bf16[37,64,128]{2,1,0:T(8,128)(2,1)S(1)}, u32[]{:S(2)}, u32[]{:S(2)}) collective-permute-start(bf16[37,64,128]{2,1,0:T(8,128)(2,1)S(1)} %get-tuple-element.63), channel_id=1, source_target_pairs={{0,2},{5,6},{10,8},{15,12},{16,18},{21,22},{26,24},{31,28}} | collective-permute-start | bytes 1818632 | tf_op jit(solution)/shard_map/ppermute | solution.py:471
  353.7 43.0 %collective-permute-start.10 = (bf16[37,64,128]{2,1,0:T(8,128)(2,1)S(1)}, bf16[37,64,128]{2,1,0:T(8,128)(2,1)S(1)}, u32[]{:S(2)}, u32[]{:S(2)}) collective-permute-start(bf16[37,64,128]{2,1,0:T(8,128)(2,1)S(1)} %get-tuple-element.60), channel_id=1, source_target_pairs={{0,3},{5,7},{10,9},{15,13},{16,19},{21,23},{26,25},{31,29}} | collective-permute-start | bytes 1818632 | tf_op jit(solution)/shard_map/ppermute | solution.py:471
  354.4 55.2 %collective-permute-start.9 = (bf16[37,64,128]{2,1,0:T(8,128)(2,1)S(1)}, bf16[37,64,128]{2,1,0:T(8,128)(2,1)S(1)}, u32[]{:S(2)}, u32[]{:S(2)}) collective-permute-start(bf16[37,64,128]{2,1,0:T(8,128)(2,1)S(1)} %get-tuple-element.61), channel_id=1, source_target_pairs={{0,2},{5,6},{10,8},{15,12},{16,18},{21,22},{26,24},{31,28}} | collective-permute-start | bytes 1818632 | tf_op jit(solution)/shard_map/ppermute | solution.py:471
  357.1 52.5 %copy-start = (s32[3]{0:T(128)S(1)}, s32[3]{0:T(128)}, u32[]{:S(2)}) copy-start(s32[3]{0:T(128)} %pad_add_fusion.where_ref) | copy-start | bytes 40

commit v2 on v1

--- a/solution.py
+++ b/solution.py
@@ -2,6 +2,7 @@
 
 import jax
 import jax.numpy as jnp
+import numpy as np
 from jax import lax
 from jax.experimental.layout import Layout, with_layout_constraint
 from jax.experimental import pallas as pl
@@ -17,17 +18,18 @@
 FAR = 1 << 20
 ROWS = 4
 LEAD = 16
-
-
-def chain_kernel(cfg, info_ref, t_ref, f_ref, b_ref, e_ref, wa_ref, ba_ref, wb_ref, bb_ref, wo_ref, bo_ref, o_ref, buf, side, sems, X, I, bias, acc, xa, xb):
-    H, W, C, whole = cfg
+KEEPS, TURN, ORDER, HALF, EDGE, FIRST = 2, 3, 4, 5, 6, 10
+
+
+def chain_kernel(cfg, info_ref, t_ref, f_ref, b_ref, e_ref, ra_ref, rb_ref, wo_ref, add_ref, o_ref, buf, side, sems, X, I, bias, acc, xa, xb, wa_ref, wb_ref):
+    H, W, C, whole, chunk = cfg
     R = ROWS
     S = W + e_ref.shape[2]
     halo = BLOCKS * (D1 + D2)
     NB = R * S
     T = 256
     BF, F32 = jnp.bfloat16, jnp.float32
-    start = info_ref[4]
+    start = pl.multiple_of(info_ref[FIRST + chunk], ROWS)
 
     def moved(source, a, b, length, q):
         return pltpu.make_async_copy(source.at[pl.ds(a, length)], buf.at[pl.ds(b, length)], sems.at[q])
@@ -49,9 +51,25 @@
     def at(row):
         return pl.multiple_of(128 + (row + halo + LEAD) * S, 128)
 
-    for k in range(BLOCKS):
-        bias[2 * k] = jnp.broadcast_to(ba_ref[k], (C, 128))
-        bias[2 * k + 1] = jnp.broadcast_to(bb_ref[k], (C, 128))
+    for k in range(2 * BLOCKS):
+        bias[k] = jnp.broadcast_to(add_ref[:, k:k + 1], (C, 128))
+
+    def weights(turned):
+        for raw, w in ((ra_ref, wa_ref), (rb_ref, wb_ref)):
+            for k in range(BLOCKS):
+                for a in range(3):
+                    for b in range(3):
+                        p, q = (b, a) if turned else (a, b)
+                        w[k, p * C:(p + 1) * C, q * C:(q + 1) * C] = raw[k, a, :, b * C:(b + 1) * C]
+
+    @pl.when(info_ref[TURN] > 0)
+    def _():
+        weights(True)
+
+    @pl.when(info_ref[TURN] == 0)
+    def _():
+        weights(False)
+
     middle.wait()
     sides.wait()
     moved(t_ref, 0, 0, halo, 1).wait()
@@ -68,10 +86,10 @@
     lax.fori_loop(0, (H + 2 * halo) // R, fill, 0)
     lane = lax.broadcasted_iota(jnp.int32, (8, NB), 1)
     col = lane % S
-    dead = ((col < halo) & (info_ref[2] > 0)) | ((col >= halo + W) & (info_ref[3] > 0))
+    dead = ((col < halo) & (info_ref[EDGE + 2] > 0)) | ((col >= halo + W) & (info_ref[EDGE + 3] > 0))
     rl = jnp.where(dead, 4 * FAR, lane // S)
-    first = jnp.where(info_ref[0] > 0, -start, -FAR)
-    last = jnp.where(info_ref[1] > 0, whole - start, FAR)
+    first = jnp.where(info_ref[EDGE] > 0, -start, -FAR)
+    last = jnp.where(info_ref[EDGE + 1] > 0, whole - start, FAR)
 
     def masked(v, row, t):
         p = rl[:, t:t + T]
@@ -122,21 +140,22 @@
         edge = (BLOCKS - k) * (D1 + D2)
 
         def emit_a(row, t, v):
-            v = biased(v, 2 * k)
+            v = biased(v, k)
             e = jnp.where(v > 0, v, jnp.exp(v) - 1.0)
             I[:, pl.ds(at(row) + t, T)] = masked(e, row, t).astype(BF)
 
         conv(X, D1, wa_ref, k, edge - D1, emit_a)
 
         def emit_b(row, t, v):
-            v = biased(v, 2 * k + 1) + X[:, pl.ds(at(row) + t, T)].astype(F32)
+            v = biased(v, BLOCKS + k) + X[:, pl.ds(at(row) + t, T)].astype(F32)
             X[:, pl.ds(at(row) + t, T)] = masked(v, row, t).astype(BF)
 
         conv(I, D2, wb_ref, k, edge - D1 - D2, emit_b)
         return carry
 
     lax.fori_loop(0, BLOCKS, block, 0)
-    bo = jnp.broadcast_to(bo_ref[...], (bo_ref.shape[0], W))
+    K = wo_ref.shape[0]
+    bo = jnp.broadcast_to(add_ref[:K, 2 * BLOCKS:2 * BLOCKS + 1], (K, W))
 
     def project(i, _):
         x = X[:, pl.ds(at(i * R), NB)]
@@ -148,23 +167,20 @@
     lax.fori_loop(0, H // R, project, 0)
 
 
-def chain(info, top, field, bottom, side, wa, ba, wb, bb, wo, bo, H):
+def chain(info, chunk, top, field, bottom, side, wa, wb, wo, add, H):
     whole, C, W = field.shape
     S = W + side.shape[2]
     K = wo.shape[0]
     R = ROWS
     halo = BLOCKS * (D1 + D2)
     N = 128 + (H + 2 * halo + LEAD + R) * S + 256
-    KP = -(-K // 16) * 16
-    wo = jnp.pad(wo, ((0, KP - K), (0, 0)))
-    bo = jnp.pad(bo, (0, KP - K))[:, None]
     vm = pl.BlockSpec(memory_space=pltpu.VMEM)
     ring = (2 * (max(D1, D2) // R) + 1) * R * S
     flops = 2 * BLOCKS * 2 * 9 * C * C * H * S
-    out = pl.pallas_call(
-        functools.partial(chain_kernel, (H, W, C, whole)),
-        out_shape=jax.ShapeDtypeStruct((H, KP, W), jnp.bfloat16),
-        in_specs=[pl.BlockSpec(memory_space=pltpu.SMEM), *[pl.BlockSpec(memory_space=pltpu.HBM)] * 4] + [vm] * 6,
+    return pl.pallas_call(
+        functools.partial(chain_kernel, (H, W, C, whole, chunk)),
+        out_shape=jax.ShapeDtypeStruct((H, K, W), jnp.bfloat16),
+        in_specs=[pl.BlockSpec(memory_space=pltpu.SMEM), *[pl.BlockSpec(memory_space=pltpu.HBM)] * 4] + [vm] * 4,
         out_specs=vm,
         scratch_shapes=[
             pltpu.VMEM((H + 2 * halo, C, W), jnp.bfloat16),
@@ -176,12 +192,13 @@
             pltpu.VMEM((C, ring), jnp.float32),
             pltpu.VMEM((2 * C, R * S), jnp.bfloat16),
             pltpu.VMEM((2 * C, R * S), jnp.bfloat16),
+            pltpu.VMEM((BLOCKS, 3 * C, 3 * C), jnp.bfloat16),
+            pltpu.VMEM((BLOCKS, 3 * C, 3 * C), jnp.bfloat16),
         ],
         compiler_params=pltpu.CompilerParams(vmem_limit_bytes=63000 * 1024),
         cost_estimate=pl.CostEstimate(flops=flops, bytes_accessed=4 * C * H * S, transcendentals=2 * C * H * S),
         name="chain",
-    )(info, top, field, bottom, side, wa, ba[:, :, None], wb, bb[:, :, None], wo, bo)
-    return out[:, :K]
+    )(info, top, field, bottom, side, wa, wb, wo, add)
 
 
 def neighbours(first, last, axis):
@@ -205,13 +222,40 @@
     return above, below, left, right, corners
 
 
+def table(rows, cols, homes, step):
+    lines = []
+    for r in range(rows):
+        for c in range(cols):
+            diagonal = 2 * (2 * r < rows) if homes else 0
+            _, turn, order = homes.get((r, c), (0, 0, diagonal))
+            edge = [r == 0, r == rows - 1, c == 0, c == cols - 1]
+            if turn:
+                edge = edge[2:] + edge[:2]
+            chunks = CHUNKS if homes else 1
+            q = cols // chunks
+            starts = [((j * q) ^ (order & ~(q - 1))) * step if homes else 0 for j in range(chunks)]
+            lines.append([r, c, r in (0, rows - 1), turn, order, order // 2, *edge, *starts])
+    return np.array(lines, np.int32)
+
+
 def shards(pair_maps, conv_a, bias_a, conv_b, bias_b, out_weight, out_bias):
     rows, cols = lax.axis_size("rows"), lax.axis_size("cols")
     _, C, H, W = pair_maps.shape
+    K = out_bias.shape[0]
     halo = BLOCKS * (D1 + D2)
-    r, c = lax.axis_index("rows"), lax.axis_index("cols")
-    edge = jnp.stack([r == 0, r == rows - 1, c == 0, c == cols - 1]).astype(jnp.int32)
+    me = lax.axis_index("rows") * cols + lax.axis_index("cols")
+    square_grid = rows == 4 and cols == 4 and H == W and H // rows == 64
+    homes = plan(cols) if square_grid else {}
+    lines = table(rows, cols, homes, H // cols)
+    info = lax.dynamic_slice(jnp.asarray(lines), (me, 0), (1, lines.shape[1]))[0]
+    add = jnp.concatenate([bias_a.T, bias_b.T, jnp.pad(out_bias, (0, C - K))[:, None]], axis=1)
     tile = pair_maps[0]
+    turn, off = info[TURN], info[ORDER]
+
+    def upright(v):
+        return jnp.transpose(v, (1, 0, 2))
+
+    field = lax.cond(turn > 0, lambda v: jnp.transpose(v, (2, 0, 1)), upright, tile) if square_grid else upright(tile)
     above, below, left, right, corners = rims(tile)
     flat = jnp.concatenate
 
@@ -220,43 +264,29 @@
         east = flat([corners[:, second], right, corners[:, 3]], axis=2)
         return west, east
 
-    def caller(top, field, bottom, west, east, wa, wb, length):
+    def caller(top, bottom, west, east, length):
         gap = jnp.zeros((C, 64 - 2 * halo, west.shape[2]), west.dtype)
         west, east, top, bottom = (with_layout_constraint(v, Layout((0, 1, 2))) for v in (west, east, top, bottom))
         side = with_layout_constraint(flat([west, east, gap], axis=1), Layout((0, 1, 2)))
         side, top, bottom = lax.optimization_barrier((side, top, bottom))
         side, top, bottom = jnp.transpose(side, (2, 0, 1)), jnp.transpose(top, (1, 0, 2)), jnp.transpose(bottom, (1, 0, 2))
-        return lambda info: chain(info, top, field, bottom, side, wa, bias_a, wb, bias_b, out_weight, out_bias, length)
+        return lambda info, j: chain(info, j, top, field, bottom, side, conv_a, conv_b, out_weight, add, length)
 
     square_grid = rows == 4 and cols == 4 and H == W and H // rows == 64
 
-    def merged(w):
-        return w.reshape(BLOCKS, 3 * C, 3 * C)
-
     if square_grid:
-        me = r * cols + c
-        homes = plan(cols)
-        turn, off = (jnp.array([homes.get((i // cols, i % cols), (0, 0, 2 * (2 * i < rows * cols)))[q] for i in range(rows * cols)])[me] for q in (1, 2))
-        field = lax.cond(turn > 0, lambda v: jnp.transpose(v, (2, 0, 1)), lambda v: jnp.transpose(v, (1, 0, 2)), tile)
         fixed = with_layout_constraint(jnp.swapaxes(corners, 2, 3), Layout((0, 1, 2, 3)))
         corners = jnp.where(turn > 0, fixed[:, jnp.array([0, 2, 1, 3])], with_layout_constraint(corners, Layout((0, 1, 2, 3))))
         north, south, west, east = (jnp.where(turn > 0, a, b) for a, b in ((left, above), (right, below), (above, left), (below, right)))
         west, east = sides(west, east, corners, 1, 2)
-        edge = jnp.where(turn > 0, edge[jnp.array([2, 3, 0, 1])], edge)
-
-        def turned(w):
-            other = jnp.transpose(w.reshape(BLOCKS, 3, C, 3, C), (0, 3, 2, 1, 4))
-            return jnp.where(turn > 0, merged(other), merged(w))
-
-        wa, wb = turned(conv_a), turned(conv_b)
         q = cols // CHUNKS
-        run = caller(north, field, south, west, east, wa, wb, H // CHUNKS)
+        run = caller(north, south, west, east, H // CHUNKS)
         chunks, strips, recs = [], [], []
         for j in range(CHUNKS):
-            info = jnp.append(edge, ((j * q) ^ (off & ~(q - 1))) * (H // cols))
+            place_of = info
             if j:
-                info, *_ = lax.optimization_barrier((info, *strips[-q:], ahead))
-            chunks.append(jnp.transpose(run(info), (1, 0, 2)))
+                place_of, *_ = lax.optimization_barrier((info, *strips[-q:], ahead))
+            chunks.append(upright(run(place_of, j)))
             for m in range(j * q, j * q + q):
                 strips.append(lax.dynamic_slice_in_dim(chunks[j], ((m % q) ^ (off & (q - 1))) * (H // cols), H // cols, 1))
                 perm = [(i * cols + k, home * cols + (m ^ o)) for (i, k), (home, _, o) in homes.items()]
@@ -264,10 +294,9 @@
             if not j:
                 ahead = own_pairs(lax.dynamic_slice_in_dim(chunks[0], (off & 2) * (H // cols), W // CHUNKS, 2))
                 early = crossing(ahead)
-        return square(chunks, strips, recs, early, off)
-    field = jnp.transpose(tile, (1, 0, 2))
+        return square(chunks, strips, recs, early, info)
     west, east = sides(left, right, corners, 1, 2)
-    logits = caller(above, field, below, west, east, merged(conv_a), merged(conv_b), H)(jnp.append(edge, 0))
+    logits = caller(above, below, west, east, H)(info, 0)
     logits = jnp.transpose(logits, (1, 0, 2))[None]
     strips = lax.all_to_all(logits, "cols", split_axis=2, concat_axis=3, tiled=True)
     flipped = lax.all_to_all(strips, ("rows", "cols"), split_axis=3, concat_axis=2, tiled=True)
@@ -278,7 +307,7 @@
 
 def pair_kernel(n, where_ref, r0, r1, r2, r3, o_ref, msg, lab, sems):
     K, sub, lanes = r0.shape
-    r, s, keeps = where_ref[0], where_ref[1], where_ref[2]
+    r, s, keeps = where_ref[0], where_ref[1], where_ref[KEEPS]
     g = pl.program_id(0)
     W = lanes * pl.num_programs(0)
 
@@ -371,7 +400,7 @@
 def place_kernel(n, where_ref, mine, other, e0, e1, l0, l1, near, far, _, o_ref, own, one, two, sems):
     K, sub, W = mine.shape
     F32 = jnp.float32
-    r, s, keeps = where_ref[0], where_ref[1], where_ref[2]
+    r, s, keeps = where_ref[0], where_ref[1], where_ref[KEEPS]
 
     def out(source, tile, q):
         spot = pl.multiple_of(lax.rem(tile, n) * W, W)
@@ -501,12 +530,12 @@
             num_scalar_prefetch=1,
             grid=(2,),
             in_specs=[
-                pl.BlockSpec((K, B, B), lambda g, h: (0, 0, (1 - h[0]) * (1 - g) + h[0] * g)),
-                pl.BlockSpec((K, B, B), lambda g, h: (0, 0, 1 - h[0])),
-                pl.BlockSpec((K, B, B), lambda g, h: (0, 0, 1 - h[0])),
+                pl.BlockSpec((K, B, B), lambda g, h: (0, 0, (1 - h[HALF]) * (1 - g) + h[HALF] * g)),
+                pl.BlockSpec((K, B, B), lambda g, h: (0, 0, 1 - h[HALF])),
+                pl.BlockSpec((K, B, B), lambda g, h: (0, 0, 1 - h[HALF])),
             ],
             out_specs=[
-                pl.BlockSpec((K, B, B), lambda g, h: (0, 0, (1 - h[0]) * (1 - g) + h[0] * g)),
+                pl.BlockSpec((K, B, B), lambda g, h: (0, 0, (1 - h[HALF]) * (1 - g) + h[HALF] * g)),
                 pl.BlockSpec((K, B, B), lambda g, h: (0, 0, 0)),
             ],
             scratch_shapes=[pltpu.VMEM((K, B, B), jnp.float32)],
@@ -517,19 +546,17 @@
     )(half, near_rows, near_rows, far_rows)
 
 
-def square(chunks, strips, recs, early, off):
+def square(chunks, strips, recs, early, info):
     n = lax.axis_size("rows")
     axes = ("rows", "cols")
     r, s = lax.axis_index("rows"), lax.axis_index("cols")
     sub = strips[0].shape[1]
     far_rows, near_rows, *_ = lax.optimization_barrier((*chunks, *strips))
-    near, far = rest_pairs((off // 2)[None].astype(jnp.int32), far_rows, near_rows)
+    near, far = rest_pairs(info, far_rows, near_rows)
     late = crossing(far)
     mine, other = (lax.dynamic_slice_in_dim(near, v * sub, sub, 1) for v in (r % 2, 1 - r % 2))
     other = lax.ppermute(other, axes, [(i * n + i, i * n + (i ^ 1)) for i in range(n)])
-    keeps = jnp.where((r == 0) | (r == n - 1), 1, 0)
-    where = jnp.stack([r, s, keeps]).astype(jnp.int32)
-    result, msg = pairs(where, recs)
+    result, msg = pairs(info, recs)
     near, far = [], []
     for k in range(n):
         t = lax.rem(s + k, n)
@@ -537,7 +564,7 @@
             payload = lax.dynamic_slice(msg, (half, t, 0, 0, 0), (1, 1) + msg.shape[2:])[0, 0]
             perm = [(i * n + j, o * n + (j + k) % n) for i, o in moves for j in range(n)]
             kept.append(lax.ppermute(payload, axes, perm))
-    return place(where, [mine, other, *early, *late], jnp.stack(near), jnp.stack(far), result)[None]
+    return place(info, [mine, other, *early, *late], jnp.stack(near), jnp.stack(far), result)[None]
 
 
 def solution(mesh):

time: 417 us -> 411 us (0.986)
  local copies, waits for them, and re-layouts: 63.3 us -> 57.8 us
    pallas_call x0 -> x4, local copies, waits for them, and re-layouts: none -> 8.65 us  [chain(): pl.pallas_call(functools.partial(chain_kernel, (H, W, C, whole, chunk)),...]
    unnamed x54 -> x28, local copies, waits for them, and re-layouts: 8.76 us -> 1.34 us
    optimization_barrier x3 -> x1, local copies, waits for them, and re-layouts: 11.5 us -> 9.31 us  [caller(): side, top, bottom = lax.optimization_barrier((side, top, bottom))]
  transfers between devices with their start and end apart: 23 -> 23, of which waited for: 9 -> 9; matrix products, arithmetic and copies ran while one was open for 10% -> 8% of each run, Pallas kernels for 18% -> 18%
where the time goes in v2:
time: 411 us; the launch traced here: 409 us
  Pallas kernels  155 us (38%)
  waiting for transfers between devices  115 us (28%)
  starting transfers between devices  63.9 us (16%)
  local copies, waits for them, and re-layouts  57.8 us (14%)
  other arithmetic  9.46 us (2%)
  matrix products  5.93 us (1%)
    pallas_call x2, Pallas kernels, chain(): pl.pallas_call(functools.partial(chain_kernel, (H, W, C, whole, chunk)),...  125 us
    ppermute x4, waiting for transfers between devices, crossing(): lax.ppermute(block[:, e * sub:(e + 1) * sub], ('rows', 'cols'), perm)  52.3 us
    ppermute x8, starting transfers between devices, square(): kept.append(lax.ppermute(payload, axes, perm))  30 us
    ppermute x4, waiting for transfers between devices, shards(): recs.append(lax.ppermute(strips[m], ('rows', 'cols'), perm))  27.1 us
    ppermute x8, waiting for transfers between devices, square(): kept.append(lax.ppermute(payload, axes, perm))  19.3 us
    ppermute x6, starting transfers between devices, neighbours(): return (lax.ppermute(last, axis, up), lax.ppermute(first, axis, down))  16.9 us
    ppermute x6, waiting for transfers between devices, neighbours(): return (lax.ppermute(last, axis, up), lax.ppermute(first, axis, down))  16.1 us
    pallas_call x1, Pallas kernels, rest_pairs(): pl.pallas_call(rest_kernel, grid_spec=pltpu.PrefetchScalarGridSpec(num_sc...  12.6 us
  transfers between devices with their start and end apart: 23, of which 9 were waited for; matrix products, arithmetic and copies ran while one was open for 8% of the time, Pallas kernels for 18%

profile of v2, /device:TPU:2, one launch (start us, length us, event | category | flops | bytes accessed | tf_op | source)
XLA Modules:
  0.0 409.2 jit_solution(15753910827453285406)
XLA Ops:
  0.0 5.9 %convolution_bitcast_fusion = bf16[64,48,256]{2,1,0:T(8,128)(2,1)S(1)} fusion(s32[48]{0:T(128)S(1)} %compare_select_fusion, bf16[1,64,256,256]{3,2,1,0:T(8,128)(2,1)} %param.11), kind=kOutput, calls=%fused_computation.3 | convolution fusion | flops 402665472 | bytes 9961664 | tf_op jit(solution)/shard_map/dq,cpq->cdp/dot_general | solution.py:217
  6.9 3.5 collective-permute-start
  10.5 2.4 fusion.5
  12.8 1.9 collective-permute-start.4
  16.0 3.6 collective-permute-start.5
  22.2 5.3 %collective-permute-done = bf16[64,24,256]{2,1,0:T(8,128)(2,1)S(1)} collective-permute-done((bf16[64,24,256]{2,1,0:T(8,128)(2,1)}, bf16[64,24,256]{2,1,0:T(8,128)(2,1)S(1)}, u32[]{:S(2)}, u32[]{:S(2)}) %collective-permute-start) | collective-permute-done | bytes 786464 | tf_op jit(solution)/shard_map/ppermute | solution.py:208
  27.5 2.6 broadcast_select_fusion.1
  30.1 4.9 %collective-permute-done.1 = bf16[64,24,256]{2,1,0:T(8,128)(2,1)S(1)} collective-permute-done((bf16[64,24,256]{2,1,0:T(8,128)(2,1)S(1)}, bf16[64,24,256]{2,1,0:T(8,128)(2,1)S(1)}, u32[]{:S(2)}, u32[]{:S(2)}) %collective-permute-start.1) | collective-permute-done | bytes 786464 | tf_op jit(solution)/shard_map/ppermute | solution.py:208
  35.0 2.6 broadcast_select_fusion
  38.6 4.4 %collective-permute-start.3 = (bf16[64,48,24]{0,2,1:T(8,128)(2,1)S(1)}, bf16[64,48,24]{0,2,1:T(8,128)(2,1)S(1)}, u32[]{:S(2)}, u32[]{:S(2)}) collective-permute-start(bf16[64,48,24]{0,2,1:T(8,128)(2,1)S(1)} %copy.31), channel_id=1, source_target_pairs={{4,0},{8,4},{12,8},{5,1},{9,5},{13,9},{6,2},{10,6},{14,10},{7,3},{... | collective-permute-start | bytes 442376 | tf_op jit(solution)/shard_map/ppermute | solution.py:208
  45.2 12.1 %conditional.1 = (bf16[256,64,256]{2,1,0:T(8,128)(2,1)}) conditional(s32[]{:T(128)} %convert_element_type.6, bf16[64,256,256]{2,1,0:T(8,128)(2,1)} %bitcast.87, (bf16[64,256,256]{2,1,0:T(8,128)(2,1)}) %tuple.49), branch_computations={%region_0.1_spmd, %region_1.2_spmd} | conditional | bytes 16777224 | solution.py:258
  45.2 12.1 %copy.52 = bf16[256,64,256]{2,1,0:T(8,128)(2,1)} copy(bf16[256,64,256]{0,2,1:T(8,128)(2,1)} %bitcast.90) | data formatting | bytes 16777216 | tf_op jit(solution)/shard_map/cond | solution.py:258
  58.0 2.1 collective-permute-start.2
  60.2 5.9 %collective-permute-done.2 = bf16[64,48,24]{0,2,1:T(8,128)(2,1)S(1)} collective-permute-done((bf16[64,48,24]{0,2,1:T(8,128)(2,1)S(1)}, bf16[64,48,24]{0,2,1:T(8,128)(2,1)S(1)}, u32[]{:S(2)}, u32[]{:S(2)}) %collective-permute-start.2) | collective-permute-done | bytes 147488 | tf_op jit(solution)/shard_map/ppermute | solution.py:208
  67.2 2.3 copy.32
  69.5 2.3 gather_fusion
  73.3 2.4 maximum_maximum_fusion
  75.7 9.3 %copy.38 = bf16[64,64,304]{1,0,2:T(8,128)(2,1)} copy(bf16[64,64,304]{2,1,0:T(8,128)(2,1)S(1)} %maximum_maximum_fusion) | data formatting | bytes 4980736 | tf_op jit(solution)/shard_map/optimization_barrier | solution.py:271
  85.0 2.9 copy_bitcast_fusion
  87.9 62.6 %chain.2 = bf16[128,37,256]{2,1,0:T(8,128)(2,1)} custom-call(s32[12]{0:T(128)} %get-tuple-element.23.info_ref.h_ref.where_ref, bf16[24,64,256]{2,1,0:T(8,128)(2,1)} %get-tuple-element.75.t_ref, bf16[256,64,256]{2,1,0:T(8,128)(2,1)} %get-tuple-element.30.f_ref, bf16[24,64,256]{2,1,0:T(8,128)(2,1)} %get-tuple-element.74.b_ref, bf16[304,64,64]{2,1,0:T(8,128)(2,1)} %bitcast.95, ...), custom_call_target="tpu_custom_call" | custom-call | flops 12079595520 | bytes 10485760 | tf_op jit(solution)/shard_map/chain/pallas_call | solution.py:180
  150.5 2.3 copy.41
  152.8 1.3 dynamic-slice_bitcast_fusion.2.a_ref.b_ref
  154.2 5.1 %own.1 = bf16[37,128,128]{2,1,0:T(8,128)(2,1)} custom-call(bf16[37,128,128]{2,1,0:T(8,128)(2,1)} %dynamic-slice_bitcast_fusion.2.a_ref.b_ref, bf16[37,128,128]{2,1,0:T(8,128)(2,1)} %dynamic-slice_bitcast_fusion.2.a_ref.b_ref), custom_call_target="tpu_custom_call" | custom-call | flops 3637248 | bytes 3637248 | tf_op jit(solution)/shard_map/own/pallas_call | solution.py:388
  159.3 1.6 dynamic-slice_bitcast_fusion.3
  160.9 1.4 collective-permute-start.12
  162.3 1.9 collective-permute-start.11
  164.2 62.7 %chain.3 = bf16[128,37,256]{2,1,0:T(8,128)(2,1)} custom-call(s32[12]{0:T(128)} %get-tuple-element.23.info_ref.h_ref.where_ref, bf16[24,64,256]{2,1,0:T(8,128)(2,1)} %get-tuple-element.75.t_ref, bf16[256,64,256]{2,1,0:T(8,128)(2,1)} %get-tuple-element.30.f_ref, bf16[24,64,256]{2,1,0:T(8,128)(2,1)} %get-tuple-element.74.b_ref, bf16[304,64,64]{2,1,0:T(8,128)(2,1)} %bitcast.96, ...), custom_call_target="tpu_custom_call" | custom-call | flops 12079595520 | bytes 10485760 | tf_op jit(solution)/shard_map/chain/pallas_call | solution.py:180
  226.9 2.3 copy.47
  229.2 1.8 dynamic-slice_bitcast_fusion
  231.0 2.4 collective-permute-start.14
  233.3 6.6 %collective-permute-start.13 = (bf16[37,64,256]{2,1,0:T(8,128)(2,1)}, bf16[37,64,256]{2,1,0:T(8,128)(2,1)}, u32[]{:S(2)}, u32[]{:S(2)}) collective-permute-start(bf16[37,64,256]{2,1,0:T(8,128)(2,1)} %get-tuple-element.45), channel_id=1, source_target_pairs={{1,2},{2,3},{3,12},{4,0},{6,6},{7,13},{8,1},{9,4},{11,10},{12,14},... | collective-permute-start | bytes 3637256 | tf_op jit(solution)/shard_map/ppermute | solution.py:293
  240.0 19.3 %collective-permute-done.14.r3 = bf16[37,64,256]{2,1,0:T(8,128)(2,1)} collective-permute-done((bf16[37,64,256]{2,1,0:T(8,128)(2,1)}, bf16[37,64,256]{2,1,0:T(8,128)(2,1)}, u32[]{:S(2)}, u32[]{:S(2)}) %collective-permute-start.14) | collective-permute-done | bytes 1212448 | tf_op jit(solution)/shard_map/ppermute | solution.py:293
  259.2 7.8 %collective-permute-done.13.r2 = bf16[37,64,256]{2,1,0:T(8,128)(2,1)} collective-permute-done((bf16[37,64,256]{2,1,0:T(8,128)(2,1)}, bf16[37,64,256]{2,1,0:T(8,128)(2,1)}, u32[]{:S(2)}, u32[]{:S(2)}) %collective-permute-start.13) | collective-permute-done | bytes 1212448 | tf_op jit(solution)/shard_map/ppermute | solution.py:293
  267.0 6.0 %pairs.1 = (f32[37,64,1024]{2,1,0:T(8,128)}, bf16[2,4,37,32,128]{4,3,2,1,0:T(8,128)(2,1)}) custom-call(s32[12]{0:T(128)} %get-tuple-element.23.info_ref.h_ref.where_ref, bf16[37,64,256]{2,1,0:T(8,128)(2,1)} %copy-done.7, bf16[37,64,256]{2,1,0:T(8,128)(2,1)} %copy-done.6, bf16[37,64,256]{2,1,0:T(8,128)(2,1)} %collective-permute-done.13.r2, ...), custom_call_target="tpu_custom_call" | custom-call | tf_op jit(solution)/shard_map/pairs/pallas_call | solution.py:351
  273.1 3.1 dynamic-slice_bitcast_fusion.8
  277.4 1.3 collective-permute-start.22
  278.8 1.3 collective-permute-start.21
  281.4 2.0 copy.60
  283.6 2.1 copy.59
  285.7 12.6 %rest.1 = (bf16[37,128,256]{2,1,0:T(8,128)(2,1)}, bf16[37,128,128]{2,1,0:T(8,128)(2,1)}) custom-call(s32[12]{0:T(128)} %get-tuple-element.23.info_ref.h_ref.where_ref, bf16[37,128,256]{2,1,0:T(8,128)(2,1)} %bitcast.91, bf16[37,128,256]{2,1,0:T(8,128)(2,1)} %bitcast.92, bf16[37,128,256]{2,1,0:T(8,128)(2,1)} %bitcast.93), custom_call_target="tpu_custom_call" | custom-call | flops 7274496 | bytes 7274496 | tf_op jit(solution)/shard_map/rest/pallas_call | solution.py:527
  298.3 2.0 constant_dynamic-slice_fusion
  301.2 24.1 %collective-permute-start.18 = (bf16[37,32,128]{2,1,0:T(8,128)(2,1)S(1)}, bf16[37,32,128]{2,1,0:T(8,128)(2,1)S(1)}, u32[]{:S(2)}, u32[]{:S(2)}) collective-permute-start(bf16[37,32,128]{2,1,0:T(8,128)(2,1)S(1)} %copy-done.9), channel_id=1, source_target_pairs={{0,7},{1,4},{2,5},{3,6},{4,11},{5,8},{6,9},{7,10},{8,15},{9,12},{1... | collective-permute-start | bytes 909320 | tf_op jit(solution)/shard_map/ppermute | solution.py:566
  326.3 6.6 %collective-permute-done.18 = bf16[37,32,128]{2,1,0:T(8,128)(2,1)S(1)} collective-permute-done((bf16[37,32,128]{2,1,0:T(8,128)(2,1)S(1)}, bf16[37,32,128]{2,1,0:T(8,128)(2,1)S(1)}, u32[]{:S(2)}, u32[]{:S(2)}) %collective-permute-start.18) | collective-permute-done | bytes 303136 | tf_op jit(solution)/shard_map/ppermute | solution.py:566
  333.6 12.7 %collective-permute-done.17 = bf16[37,32,128]{2,1,0:T(8,128)(2,1)S(1)} collective-permute-done((bf16[37,32,128]{2,1,0:T(8,128)(2,1)S(1)}, bf16[37,32,128]{2,1,0:T(8,128)(2,1)S(1)}, u32[]{:S(2)}, u32[]{:S(2)}) %collective-permute-start.17) | collective-permute-done | bytes 303136 | tf_op jit(solution)/shard_map/ppermute | solution.py:566
  349.6 1.4 pad_maximum_fusion.1.far
  351.2 39.3 %collective-permute-done.7.e0 = bf16[37,64,128]{2,1,0:T(8,128)(2,1)S(1)} collective-permute-done((bf16[37,64,128]{2,1,0:T(8,128)(2,1)S(1)}, bf16[37,64,128]{2,1,0:T(8,128)(2,1)S(1)}, u32[]{:S(2)}, u32[]{:S(2)}) %collective-permute-start.7) | collective-permute-done | bytes 606240 | tf_op jit(solution)/shard_map/ppermute | solution.py:500
  390.5 13.0 %collective-permute-done.9.l0 = bf16[37,64,128]{2,1,0:T(8,128)(2,1)S(1)} collective-permute-done((bf16[37,64,128]{2,1,0:T(8,128)(2,1)S(1)}, bf16[37,64,128]{2,1,0:T(8,128)(2,1)S(1)}, u32[]{:S(2)}, u32[]{:S(2)}) %collective-permute-start.9) | collective-permute-done | bytes 606240 | tf_op jit(solution)/shard_map/ppermute | solution.py:500
  403.5 5.5 %place.1 = f32[37,64,1024]{2,1,0:T(8,128)} custom-call(s32[12]{0:T(128)S(1)} %copy-done, bf16[37,64,256]{2,1,0:T(8,128)(2,1)S(1)} %get-tuple-element.43.mine, bf16[37,64,256]{2,1,0:T(8,128)(2,1)S(1)} %collective-permute-done.6.other, bf16[37,64,128]{2,1,0:T(8,128)(2,1)S(1)} %collective-permute-done.7.e0, ...), custom_call_target="tpu_custom_call", output_to_operand_aliasing={{}: (9, {})} | custom-call | tf_op jit(solution)/shard_map/place/pallas_call | solution.py:467
  (75 shorter events, 18.1 us)
Async XLA Ops:
  6.9 20.6 %collective-permute-start = (bf16[64,24,256]{2,1,0:T(8,128)(2,1)}, bf16[64,24,256]{2,1,0:T(8,128)(2,1)S(1)}, u32[]{:S(2)}, u32[]{:S(2)}) collective-permute-start(bf16[64,24,256]{2,1,0:T(8,128)(2,1)} %get-tuple-element.59), channel_id=1, source_target_pairs={{0,1},{1,2},{2,3},{4,5},{5,6},{6,7},{8,9},{9,10},{10,11},{12,13},{... | collective-permute-start | bytes 2359304 | tf_op jit(solution)/shard_map/ppermute | solution.py:208
  10.4 11.7 %copy-start.13 = (f32[37]{0:T(128)S(1)}, f32[37]{0:T(128)}, u32[]{:S(2)}) copy-start(f32[37]{0:T(128)} %param.17) | copy-start | bytes 448
  12.8 14.7 %collective-permute-start.4 = (bf16[64,24,256]{2,1,0:T(8,128)(2,1)}, bf16[64,24,256]{2,1,0:T(8,128)(2,1)}, u32[]{:S(2)}, u32[]{:S(2)}) collective-permute-start(bf16[64,24,256]{2,1,0:T(8,128)(2,1)} %get-tuple-element.32), channel_id=1, source_target_pairs={{0,4},{4,8},{8,12},{1,5},{5,9},{9,13},{2,6},{6,10},{10,14},{3,7},{... | collective-permute-start | bytes 2359304 | tf_op jit(solution)/shard_map/ppermute | solution.py:208
  14.7 20.3 %collective-permute-start.1 = (bf16[64,24,256]{2,1,0:T(8,128)(2,1)S(1)}, bf16[64,24,256]{2,1,0:T(8,128)(2,1)S(1)}, u32[]{:S(2)}, u32[]{:S(2)}) collective-permute-start(bf16[64,24,256]{2,1,0:T(8,128)(2,1)S(1)} %get-tuple-element.58), channel_id=1, source_target_pairs={{1,0},{2,1},{3,2},{5,4},{6,5},{7,6},{9,8},{10,9},{11,10},{13,12},{... | collective-permute-start | bytes 2359304 | tf_op jit(solution)/shard_map/ppermute | solution.py:208
  16.0 19.0 %collective-permute-start.5 = (bf16[64,24,256]{2,1,0:T(8,128)(2,1)S(1)}, bf16[64,24,256]{2,1,0:T(8,128)(2,1)}, u32[]{:S(2)}, u32[]{:S(2)}) collective-permute-start(bf16[64,24,256]{2,1,0:T(8,128)(2,1)S(1)} %get-tuple-element.33), channel_id=1, source_target_pairs={{4,0},{8,4},{12,8},{5,1},{9,5},{13,9},{6,2},{10,6},{14,10},{7,3},{... | collective-permute-start | bytes 2359304 | tf_op jit(solution)/shard_map/ppermute | solution.py:208
  37.6 5.4 %copy-start.10 = (f32[2,64]{1,0:T(2,128)S(1)}, f32[2,64]{1,0:T(2,128)}, u32[]{:S(2)}) copy-start(f32[2,64]{1,0:T(2,128)} %param.15) | copy-start | bytes 1540
  37.6 5.4 %copy-start.11 = (f32[2,64]{1,0:T(2,128)S(1)}, f32[2,64]{1,0:T(2,128)}, u32[]{:S(2)}) copy-start(f32[2,64]{1,0:T(2,128)} %param.13) | copy-start | bytes 1540
  38.6 21.5 %collective-permute-start.3 = (bf16[64,48,24]{0,2,1:T(8,128)(2,1)S(1)}, bf16[64,48,24]{0,2,1:T(8,128)(2,1)S(1)}, u32[]{:S(2)}, u32[]{:S(2)}) collective-permute-start(bf16[64,48,24]{0,2,1:T(8,128)(2,1)S(1)} %copy.31), channel_id=1, source_target_pairs={{4,0},{8,4},{12,8},{5,1},{9,5},{13,9},{6,2},{10,6},{14,10},{7,3},{... | collective-permute-start | bytes 442376 | tf_op jit(solution)/shard_map/ppermute | solution.py:208
  45.2 12.2 %copy-start.12 = (s32[4]{0:T(128)S(1)}, s32[4]{0:T(128)}, u32[]{:S(2)}) copy-start(s32[4]{0:T(128)} %constant.81) | copy-start | bytes 52
  58.0 8.0 %collective-permute-start.2 = (bf16[64,48,24]{0,2,1:T(8,128)(2,1)S(1)}, bf16[64,48,24]{0,2,1:T(8,128)(2,1)S(1)}, u32[]{:S(2)}, u32[]{:S(2)}) collective-permute-start(bf16[64,48,24]{0,2,1:T(8,128)(2,1)S(1)} %copy.30), channel_id=1, source_target_pairs={{0,4},{4,8},{8,12},{1,5},{5,9},{9,13},{2,6},{6,10},{10,14},{3,7},{... | collective-permute-start | bytes 442376 | tf_op jit(solution)/shard_map/ppermute | solution.py:208
  71.9 1.1 copy-start.4
  71.9 1.4 copy-start.5
  160.9 79.0 %collective-permute-start.12 = (bf16[37,64,256]{2,1,0:T(8,128)(2,1)}, bf16[37,64,256]{2,1,0:T(8,128)(2,1)S(1)}, u32[]{:S(2)}, u32[]{:S(2)}) collective-permute-start(bf16[37,64,256]{2,1,0:T(8,128)(2,1)} %get-tuple-element.46), channel_id=1, source_target_pairs={{1,1},{2,0},{3,15},{4,3},{6,5},{7,14},{8,2},{9,7},{11,9},{12,13},{... | collective-permute-start | bytes 3637256 | tf_op jit(solution)/shard_map/ppermute | solution.py:293
  162.3 77.7 %collective-permute-start.11 = (bf16[37,64,256]{2,1,0:T(8,128)(2,1)}, bf16[37,64,256]{2,1,0:T(8,128)(2,1)S(1)}, u32[]{:S(2)}, u32[]{:S(2)}) collective-permute-start(bf16[37,64,256]{2,1,0:T(8,128)(2,1)} %get-tuple-element.47), channel_id=1, source_target_pairs={{1,0},{2,1},{3,14},{4,2},{6,4},{7,15},{8,3},{9,6},{11,8},{12,12},{... | collective-permute-start | bytes 3637256 | tf_op jit(solution)/shard_map/ppermute | solution.py:293
  231.0 28.3 %collective-permute-start.14 = (bf16[37,64,256]{2,1,0:T(8,128)(2,1)}, bf16[37,64,256]{2,1,0:T(8,128)(2,1)}, u32[]{:S(2)}, u32[]{:S(2)}) collective-permute-start(bf16[37,64,256]{2,1,0:T(8,128)(2,1)} %get-tuple-element.44), channel_id=1, source_target_pairs={{1,3},{2,2},{3,13},{4,1},{6,7},{7,12},{8,0},{9,5},{11,11},{12,15},... | collective-permute-start | bytes 3637256 | tf_op jit(solution)/shard_map/ppermute | solution.py:293
  233.3 33.7 %collective-permute-start.13 = (bf16[37,64,256]{2,1,0:T(8,128)(2,1)}, bf16[37,64,256]{2,1,0:T(8,128)(2,1)}, u32[]{:S(2)}, u32[]{:S(2)}) collective-permute-start(bf16[37,64,256]{2,1,0:T(8,128)(2,1)} %get-tuple-element.45), channel_id=1, source_target_pairs={{1,2},{2,3},{3,12},{4,0},{6,6},{7,13},{8,1},{9,4},{11,10},{12,14},... | collective-permute-start | bytes 3637256 | tf_op jit(solution)/shard_map/ppermute | solution.py:293
  239.9 27.1 %copy-start.6 = (bf16[37,64,256]{2,1,0:T(8,128)(2,1)}, bf16[37,64,256]{2,1,0:T(8,128)(2,1)S(1)}, u32[]{:S(2)}) copy-start(bf16[37,64,256]{2,1,0:T(8,128)(2,1)S(1)} %collective-permute-done.12.r1) | copy-start | bytes 3637252
  240.0 27.1 %copy-start.7 = (bf16[37,64,256]{2,1,0:T(8,128)(2,1)}, bf16[37,64,256]{2,1,0:T(8,128)(2,1)S(1)}, u32[]{:S(2)}) copy-start(bf16[37,64,256]{2,1,0:T(8,128)(2,1)S(1)} %collective-permute-done.11.r0) | copy-start | bytes 3637252
  273.0 8.3 %copy-start.1 = (bf16[128,37,256]{2,1,0:T(8,128)(2,1)S(1)}, bf16[128,37,256]{2,1,0:T(8,128)(2,1)}, u32[]{:S(2)}) copy-start(bf16[128,37,256]{2,1,0:T(8,128)(2,1)} %chain.2) | copy-start | bytes 7274500
  276.2 25.0 %collective-permute-start.19 = (bf16[37,32,128]{2,1,0:T(8,128)(2,1)}, bf16[37,32,128]{2,1,0:T(8,128)(2,1)}, u32[]{:S(2)}, u32[]{:S(2)}) collective-permute-start(bf16[37,32,128]{2,1,0:T(8,128)(2,1)} %get-tuple-element.34), channel_id=1, source_target_pairs={{0,8},{1,9},{2,10},{3,11},{12,4},{13,5},{14,6},{15,7},{16,24},{17,... | collective-permute-start | bytes 909320 | tf_op jit(solution)/shard_map/ppermute | solution.py:566
  277.4 47.8 %collective-permute-start.22 = (bf16[37,32,128]{2,1,0:T(8,128)(2,1)}, bf16[37,32,128]{2,1,0:T(8,128)(2,1)}, u32[]{:S(2)}, u32[]{:S(2)}) collective-permute-start(bf16[37,32,128]{2,1,0:T(8,128)(2,1)} %get-tuple-element.35), channel_id=1, source_target_pairs={{0,11},{1,8},{2,9},{3,10},{12,7},{13,4},{14,5},{15,6},{16,27},{17,... | collective-permute-start | bytes 909320 | tf_op jit(solution)/shard_map/ppermute | solution.py:566
  278.8 46.5 %collective-permute-start.21 = (bf16[37,32,128]{2,1,0:T(8,128)(2,1)}, bf16[37,32,128]{2,1,0:T(8,128)(2,1)}, u32[]{:S(2)}, u32[]{:S(2)}) collective-permute-start(bf16[37,32,128]{2,1,0:T(8,128)(2,1)} %get-tuple-element.36), channel_id=1, source_target_pairs={{0,10},{1,11},{2,8},{3,9},{12,6},{13,7},{14,4},{15,5},{16,26},{17,... | collective-permute-start | bytes 909320 | tf_op jit(solution)/shard_map/ppermute | solution.py:566
  280.1 45.8 %collective-permute-start.20 = (bf16[37,32,128]{2,1,0:T(8,128)(2,1)}, bf16[37,32,128]{2,1,0:T(8,128)(2,1)}, u32[]{:S(2)}, u32[]{:S(2)}) collective-permute-start(bf16[37,32,128]{2,1,0:T(8,128)(2,1)} %get-tuple-element.37), channel_id=1, source_target_pairs={{0,9},{1,10},{2,11},{3,8},{12,5},{13,6},{14,7},{15,4},{16,25},{17,... | collective-permute-start | bytes 909320 | tf_op jit(solution)/shard_map/ppermute | solution.py:566
  281.4 2.2 copy-start.2
  298.3 2.9 copy-start.9
  298.3 27.8 %copy-start.3 = (bf16[37,128,128]{2,1,0:T(8,128)(2,1)S(1)}, bf16[37,128,128]{2,1,0:T(8,128)(2,1)}, u32[]{:S(2)}) copy-start(bf16[37,128,128]{2,1,0:T(8,128)(2,1)} %own.1) | copy-start | bytes 3637252
  300.3 25.9 %copy-start.8 = (bf16[37,128,128]{2,1,0:T(8,128)(2,1)S(1)}, bf16[37,128,128]{2,1,0:T(8,128)(2,1)}, u32[]{:S(2)}) copy-start(bf16[37,128,128]{2,1,0:T(8,128)(2,1)} %get-tuple-element.27) | copy-start | bytes 3637252
  300.3 103.2 %collective-permute-start.6 = (bf16[37,64,256]{2,1,0:T(8,128)(2,1)S(1)}, bf16[37,64,256]{2,1,0:T(8,128)(2,1)S(1)}, u32[]{:S(2)}, u32[]{:S(2)}) collective-permute-start(bf16[37,64,256]{2,1,0:T(8,128)(2,1)S(1)} %get-tuple-element.42), channel_id=1, source_target_pairs={{0,1},{5,4},{10,11},{15,14},{16,17},{21,20},{26,27},{31,30}} | collective-permute-start | bytes 3637256 | tf_op jit(solution)/shard_map/ppermute | solution.py:558
  301.2 31.7 %collective-permute-start.18 = (bf16[37,32,128]{2,1,0:T(8,128)(2,1)S(1)}, bf16[37,32,128]{2,1,0:T(8,128)(2,1)S(1)}, u32[]{:S(2)}, u32[]{:S(2)}) collective-permute-start(bf16[37,32,128]{2,1,0:T(8,128)(2,1)S(1)} %copy-done.9), channel_id=1, source_target_pairs={{0,7},{1,4},{2,5},{3,6},{4,11},{5,8},{6,9},{7,10},{8,15},{9,12},{1... | collective-permute-start | bytes 909320 | tf_op jit(solution)/shard_map/ppermute | solution.py:566
  325.3 21.0 %collective-permute-start.17 = (bf16[37,32,128]{2,1,0:T(8,128)(2,1)S(1)}, bf16[37,32,128]{2,1,0:T(8,128)(2,1)S(1)}, u32[]{:S(2)}, u32[]{:S(2)}) collective-permute-start(bf16[37,32,128]{2,1,0:T(8,128)(2,1)S(1)} %get-tuple-element.39), channel_id=1, source_target_pairs={{0,6},{1,7},{2,4},{3,5},{4,10},{5,11},{6,8},{7,9},{8,14},{9,15},{1... | collective-permute-start | bytes 909320 | tf_op jit(solution)/shard_map/ppermute | solution.py:566
  325.3 22.3 %collective-permute-start.16 = (bf16[37,32,128]{2,1,0:T(8,128)(2,1)S(1)}, bf16[37,32,128]{2,1,0:T(8,128)(2,1)S(1)}, u32[]{:S(2)}, u32[]{:S(2)}) collective-permute-start(bf16[37,32,128]{2,1,0:T(8,128)(2,1)S(1)} %get-tuple-element.40), channel_id=1, source_target_pairs={{0,5},{1,6},{2,7},{3,4},{4,9},{5,10},{6,11},{7,8},{8,13},{9,14},{1... | collective-permute-start | bytes 909320 | tf_op jit(solution)/shard_map/ppermute | solution.py:566
  325.8 22.5 %collective-permute-start.15 = (bf16[37,32,128]{2,1,0:T(8,128)(2,1)S(1)}, bf16[37,32,128]{2,1,0:T(8,128)(2,1)S(1)}, u32[]{:S(2)}, u32[]{:S(2)}) collective-permute-start(bf16[37,32,128]{2,1,0:T(8,128)(2,1)S(1)} %get-tuple-element.41), channel_id=1, source_target_pairs={{0,4},{1,5},{2,6},{3,7},{4,8},{5,9},{6,10},{7,11},{8,12},{9,13},{1... | collective-permute-start | bytes 909320 | tf_op jit(solution)/shard_map/ppermute | solution.py:566
  332.9 18.3 %collective-permute-start.8 = (bf16[37,64,128]{2,1,0:T(8,128)(2,1)S(1)}, bf16[37,64,128]{2,1,0:T(8,128)(2,1)S(1)}, u32[]{:S(2)}, u32[]{:S(2)}) collective-permute-start(bf16[37,64,128]{2,1,0:T(8,128)(2,1)S(1)} %get-tuple-element.62), channel_id=1, source_target_pairs={{0,3},{5,7},{10,9},{15,13},{16,19},{21,23},{26,25},{31,29}} | collective-permute-start | bytes 1818632 | tf_op jit(solution)/shard_map/ppermute | solution.py:500
  346.3 44.2 %collective-permute-start.7 = (bf16[37,64,128]{2,1,0:T(8,128)(2,1)S(1)}, bf16[37,64,128]{2,1,0:T(8,128)(2,1)S(1)}, u32[]{:S(2)}, u32[]{:S(2)}) collective-permute-start(bf16[37,64,128]{2,1,0:T(8,128)(2,1)S(1)} %get-tuple-element.63), channel_id=1, source_target_pairs={{0,2},{5,6},{10,8},{15,12},{16,18},{21,22},{26,24},{31,28}} | collective-permute-start | bytes 1818632 | tf_op jit(solution)/shard_map/ppermute | solution.py:500
  347.6 42.9 %collective-permute-start.10 = (bf16[37,64,128]{2,1,0:T(8,128)(2,1)S(1)}, bf16[37,64,128]{2,1,0:T(8,128)(2,1)S(1)}, u32[]{:S(2)}, u32[]{:S(2)}) collective-permute-start(bf16[37,64,128]{2,1,0:T(8,128)(2,1)S(1)} %get-tuple-element.60), channel_id=1, source_target_pairs={{0,3},{5,7},{10,9},{15,13},{16,19},{21,23},{26,25},{31,29}} | collective-permute-start | bytes 1818632 | tf_op jit(solution)/shard_map/ppermute | solution.py:500
  348.3 55.1 %collective-permute-start.9 = (bf16[37,64,128]{2,1,0:T(8,128)(2,1)S(1)}, bf16[37,64,128]{2,1,0:T(8,128)(2,1)S(1)}, u32[]{:S(2)}, u32[]{:S(2)}) collective-permute-start(bf16[37,64,128]{2,1,0:T(8,128)(2,1)S(1)} %get-tuple-element.61), channel_id=1, source_target_pairs={{0,2},{5,6},{10,8},{15,12},{16,18},{21,22},{26,24},{31,28}} | collective-permute-start | bytes 1818632 | tf_op jit(solution)/shard_map/ppermute | solution.py:500
  351.0 52.5 %copy-start = (s32[12]{0:T(128)S(1)}, s32[12]{0:T(128)}, u32[]{:S(2)}) copy-start(s32[12]{0:T(128)} %get-tuple-element.23.info_ref.h_ref.where_ref) | copy-start | bytes 148

commit v3 on v2

--- a/solution.py
+++ b/solution.py
@@ -18,7 +18,7 @@
 FAR = 1 << 20
 ROWS = 4
 LEAD = 16
-KEEPS, TURN, ORDER, HALF, EDGE, FIRST = 2, 3, 4, 5, 6, 10
+KEEPS, TURN, ORDER, HALF, EDGE, PARTNER, MAIN, FIRST = 2, 3, 4, 5, 6, 10, 11, 12
 
 
 def chain_kernel(cfg, info_ref, t_ref, f_ref, b_ref, e_ref, ra_ref, rb_ref, wo_ref, add_ref, o_ref, buf, side, sems, X, I, bias, acc, xa, xb, wa_ref, wb_ref):
@@ -234,7 +234,13 @@
             chunks = CHUNKS if homes else 1
             q = cols // chunks
             starts = [((j * q) ^ (order & ~(q - 1))) * step if homes else 0 for j in range(chunks)]
-            lines.append([r, c, r in (0, rows - 1), turn, order, order // 2, *edge, *starts])
+            apart = main = 0
+            if homes:
+                after = (r + 1) % rows
+                first, second = homes[r, after][2], homes[after, r][2]
+                apart = first ^ second
+                main = (c ^ first) >> 1 if apart == 1 else (c ^ first) & 1
+            lines.append([r, c, r in (0, rows - 1), turn, order, order // 2, *edge, apart == 2, main, *starts])
     return np.array(lines, np.int32)
 
 
@@ -307,7 +313,8 @@
 
 def pair_kernel(n, where_ref, r0, r1, r2, r3, o_ref, msg, lab, sems):
     K, sub, lanes = r0.shape
-    r, s, keeps = where_ref[0], where_ref[1], where_ref[KEEPS]
+    r, keeps, main = where_ref[0], where_ref[KEEPS], where_ref[MAIN]
+    apart = where_ref[PARTNER] > 0
     g = pl.program_id(0)
     W = lanes * pl.num_programs(0)
 
@@ -315,10 +322,11 @@
         spot = pl.multiple_of(lax.rem(tile, n) * W + g * lanes, lanes)
         return pltpu.make_async_copy(lab.at[p], o_ref.at[:, :, pl.ds(spot, lanes)], sems.at[p])
 
-    for p, (one, two) in enumerate(((r0, r2), (r1, r3))):
+    for p, (one, two, far) in enumerate(((r0, r1, r2), (r3, r2, r1))):
         total = jnp.zeros((sub, lanes), jnp.float32)
         for k in range(K):
-            v = (one[k].astype(jnp.float32) + two[k].astype(jnp.float32)) * 0.5
+            other = jnp.where(apart, far[k].astype(jnp.float32), two[k].astype(jnp.float32))
+            v = (one[k].astype(jnp.float32) + other) * 0.5
             lab[p, k] = v
             total = total + jnp.exp(v)
         norm = jnp.log(total)
@@ -330,17 +338,17 @@
                 b = w[t * sub:(t + 1) * sub]
                 msg[p, t, k] = jnp.concatenate([b[:sub // 2], b[sub // 2:]], axis=1).astype(jnp.bfloat16)
 
-        @pl.when(lax.rem(s, 2) == p)
+        @pl.when(main == p)
         def _(p=p):
             out(p, r + 1).start()
 
-        @pl.when((lax.rem(s, 2) != p) & (keeps > 0))
+        @pl.when((main != p) & (keeps > 0))
         def _(p=p):
             out(p, r + 2).start()
 
     for p in range(2):
 
-        @pl.when((lax.rem(s, 2) == p) | (keeps > 0))
+        @pl.when((main == p) | (keeps > 0))
         def _(p=p):
             out(p, 0).wait()
 
@@ -476,18 +484,18 @@
     )(where, *diag, near, far, result)
 
 
+ORDERS = {
+    (0, 1): 2, (1, 0): 3, (0, 2): 0, (2, 0): 1, (1, 2): 2, (2, 1): 3,
+    (2, 3): 0, (3, 2): 1, (3, 0): 2, (0, 3): 0, (3, 1): 3, (1, 3): 1,
+}
+
+
 def plan(n):
     homes = {}
-    for r in range(n):
-        for c in range(n):
-            gap = (c - r) % n
-            if gap == 1:
-                homes[r, c] = (r, 0, 0)
-            elif gap == 3:
-                homes[r, c] = (c, 1, 2)
-            elif gap == 2:
-                owner = 0 if 0 in (r, c) else 3
-                homes[r, c] = (owner, int(r != owner), 1 if r == owner else 3)
+    for (r, c), order in ORDERS.items():
+        gap = (c - r) % n
+        owner = r if gap == 1 else c if gap == n - 1 else 0 if 0 in (r, c) else n - 1
+        homes[r, c] = (owner, int(owner != r), order)
     return homes
 
 
@@ -560,7 +568,7 @@
     near, far = [], []
     for k in range(n):
         t = lax.rem(s + k, n)
-        for half, kept, moves in ((lax.rem(s, 2), near, [(i, (i + 1) % n) for i in range(n)]), (1 - lax.rem(s, 2), far, [(0, 2), (3, 1)])):
+        for half, kept, moves in ((info[MAIN], near, [(i, (i + 1) % n) for i in range(n)]), (1 - info[MAIN], far, [(0, 2), (3, 1)])):
             payload = lax.dynamic_slice(msg, (half, t, 0, 0, 0), (1, 1) + msg.shape[2:])[0, 0]
             perm = [(i * n + j, o * n + (j + k) % n) for i, o in moves for j in range(n)]
             kept.append(lax.ppermute(payload, axes, perm))

time: 411 us -> 401 us (0.976)
  the two profiles are of different devices: /device:TPU:2 before, /device:TPU:17 now
where the time goes in v3:
time: 401 us; the launch traced here: 399 us
  Pallas kernels  155 us (39%)
  waiting for transfers between devices  107 us (27%)
  starting transfers between devices  57.9 us (14%)
  local copies, waits for them, and re-layouts  57.2 us (14%)
  other arithmetic  9.46 us (2%)
  matrix products  5.93 us (1%)
  between operations  5.89 us (1%)
    pallas_call x2, Pallas kernels, chain(): pl.pallas_call(functools.partial(chain_kernel, (H, W, C, whole, chunk)),...  125 us
    ppermute x4, waiting for transfers between devices, crossing(): lax.ppermute(block[:, e * sub:(e + 1) * sub], ('rows', 'cols'), perm)  48.7 us
    ppermute x8, starting transfers between devices, square(): kept.append(lax.ppermute(payload, axes, perm))  25.9 us
    ppermute x4, waiting for transfers between devices, shards(): recs.append(lax.ppermute(strips[m], ('rows', 'cols'), perm))  23.8 us
    ppermute x8, waiting for transfers between devices, square(): kept.append(lax.ppermute(payload, axes, perm))  19.6 us
    ppermute x6, starting transfers between devices, neighbours(): return (lax.ppermute(last, axis, up), lax.ppermute(first, axis, down))  16.9 us
    ppermute x6, waiting for transfers between devices, neighbours(): return (lax.ppermute(last, axis, up), lax.ppermute(first, axis, down))  15.3 us
    pallas_call x1, Pallas kernels, rest_pairs(): pl.pallas_call(rest_kernel, grid_spec=pltpu.PrefetchScalarGridSpec(num_sc...  12.6 us
  transfers between devices with their start and end apart: 23, of which 9 were waited for; matrix products, arithmetic and copies ran while one was open for 8% of the time, Pallas kernels for 19%

profile of v3, /device:TPU:17, one launch (start us, length us, event | category | flops | bytes accessed | tf_op | source)
XLA Modules:
  0.0 398.9 jit_solution(7379167687228215718)
XLA Ops:
  0.0 5.9 %convolution_bitcast_fusion = bf16[64,48,256]{2,1,0:T(8,128)(2,1)S(1)} fusion(s32[48]{0:T(128)S(1)} %compare_select_fusion, bf16[1,64,256,256]{3,2,1,0:T(8,128)(2,1)} %param.11), kind=kOutput, calls=%fused_computation.3 | convolution fusion | flops 402665472 | bytes 9961664 | tf_op jit(solution)/shard_map/dq,cpq->cdp/dot_general | solution.py:217
  6.9 3.2 collective-permute-start
  10.1 2.4 fusion.5
  12.5 3.9 collective-permute-start.4
  16.5 2.1 collective-permute-start.1
  18.5 1.9 collective-permute-start.5
  23.0 4.5 %collective-permute-done = bf16[64,24,256]{2,1,0:T(8,128)(2,1)S(1)} collective-permute-done((bf16[64,24,256]{2,1,0:T(8,128)(2,1)}, bf16[64,24,256]{2,1,0:T(8,128)(2,1)S(1)}, u32[]{:S(2)}, u32[]{:S(2)}) %collective-permute-start) | collective-permute-done | bytes 786464 | tf_op jit(solution)/shard_map/ppermute | solution.py:208
  27.4 2.6 broadcast_select_fusion.1
  30.0 7.5 %collective-permute-done.1 = bf16[64,24,256]{2,1,0:T(8,128)(2,1)S(1)} collective-permute-done((bf16[64,24,256]{2,1,0:T(8,128)(2,1)S(1)}, bf16[64,24,256]{2,1,0:T(8,128)(2,1)S(1)}, u32[]{:S(2)}, u32[]{:S(2)}) %collective-permute-start.1) | collective-permute-done | bytes 786464 | tf_op jit(solution)/shard_map/ppermute | solution.py:208
  37.5 2.6 broadcast_select_fusion
  41.1 2.3 collective-permute-start.3
  45.6 11.6 %conditional.1 = (bf16[256,64,256]{2,1,0:T(8,128)(2,1)}) conditional(s32[]{:T(128)} %convert_element_type.6, bf16[64,256,256]{2,1,0:T(8,128)(2,1)} %bitcast.88, (bf16[64,256,256]{2,1,0:T(8,128)(2,1)}) %tuple.50), branch_computations={%region_0.1_spmd, %region_1.2_spmd} | conditional | bytes 16777224 | solution.py:264
  45.6 11.6 %copy.51 = bf16[256,64,256]{2,1,0:T(8,128)(2,1)} copy(bf16[256,64,256]{2,0,1:T(8,128)(2,1)} %bitcast.90) | data formatting | bytes 16777216 | tf_op jit(solution)/shard_map/cond | solution.py:264
  57.8 3.4 collective-permute-start.2
  61.3 3.4 collective-permute-done.2
  65.9 2.3 copy.32
  68.1 2.3 gather_fusion
  72.0 2.4 maximum_maximum_fusion
  74.4 9.3 %copy.38 = bf16[64,64,304]{1,0,2:T(8,128)(2,1)} copy(bf16[64,64,304]{2,1,0:T(8,128)(2,1)S(1)} %maximum_maximum_fusion) | data formatting | bytes 4980736 | tf_op jit(solution)/shard_map/optimization_barrier | solution.py:277
  83.7 2.9 copy_bitcast_fusion
  86.6 62.6 %chain.2 = bf16[128,37,256]{2,1,0:T(8,128)(2,1)} custom-call(s32[14]{0:T(128)} %get-tuple-element.23.info_ref.h_ref.where_ref, bf16[24,64,256]{2,1,0:T(8,128)(2,1)} %get-tuple-element.76.t_ref, bf16[256,64,256]{2,1,0:T(8,128)(2,1)} %get-tuple-element.30.f_ref, bf16[24,64,256]{2,1,0:T(8,128)(2,1)} %get-tuple-element.75.b_ref, bf16[304,64,64]{2,1,0:T(8,128)(2,1)} %bitcast.96, ...), custom_call_target="tpu_custom_call" | custom-call | flops 12079595520 | bytes 10485760 | tf_op jit(solution)/shard_map/chain/pallas_call | solution.py:180
  149.2 2.3 copy.41
  151.5 1.3 dynamic-slice_bitcast_fusion.2.a_ref.b_ref
  152.8 5.1 %own.1 = bf16[37,128,128]{2,1,0:T(8,128)(2,1)} custom-call(bf16[37,128,128]{2,1,0:T(8,128)(2,1)} %dynamic-slice_bitcast_fusion.2.a_ref.b_ref, bf16[37,128,128]{2,1,0:T(8,128)(2,1)} %dynamic-slice_bitcast_fusion.2.a_ref.b_ref), custom_call_target="tpu_custom_call" | custom-call | flops 3637248 | bytes 3637248 | tf_op jit(solution)/shard_map/own/pallas_call | solution.py:396
  158.0 1.6 dynamic-slice_bitcast_fusion.3
  159.6 1.9 collective-permute-start.12
  161.5 1.9 collective-permute-start.11
  163.5 62.7 %chain.3 = bf16[128,37,256]{2,1,0:T(8,128)(2,1)} custom-call(s32[14]{0:T(128)} %get-tuple-element.23.info_ref.h_ref.where_ref, bf16[24,64,256]{2,1,0:T(8,128)(2,1)} %get-tuple-element.76.t_ref, bf16[256,64,256]{2,1,0:T(8,128)(2,1)} %get-tuple-element.30.f_ref, bf16[24,64,256]{2,1,0:T(8,128)(2,1)} %get-tuple-element.75.b_ref, bf16[304,64,64]{2,1,0:T(8,128)(2,1)} %bitcast.97, ...), custom_call_target="tpu_custom_call" | custom-call | flops 12079595520 | bytes 10485760 | tf_op jit(solution)/shard_map/chain/pallas_call | solution.py:180
  226.1 2.3 copy.47
  228.4 1.8 dynamic-slice_bitcast_fusion
  230.2 2.4 collective-permute-start.14
  232.5 4.1 %collective-permute-start.13 = (bf16[37,64,256]{2,1,0:T(8,128)(2,1)}, bf16[37,64,256]{2,1,0:T(8,128)(2,1)}, u32[]{:S(2)}, u32[]{:S(2)}) collective-permute-start(bf16[37,64,256]{2,1,0:T(8,128)(2,1)} %get-tuple-element.45), channel_id=1, source_target_pairs={{1,0},{4,1},{2,2},{8,3},{6,4},{9,5},{11,10},{14,11},{12,12},{3,14}... | collective-permute-start | bytes 3637256 | tf_op jit(solution)/shard_map/ppermute | solution.py:299
  239.9 10.7 %collective-permute-done.14.r3 = bf16[37,64,256]{2,1,0:T(8,128)(2,1)} collective-permute-done((bf16[37,64,256]{2,1,0:T(8,128)(2,1)}, bf16[37,64,256]{2,1,0:T(8,128)(2,1)}, u32[]{:S(2)}, u32[]{:S(2)}) %collective-permute-start.14) | collective-permute-done | bytes 1212448 | tf_op jit(solution)/shard_map/ppermute | solution.py:299
  250.6 13.0 %collective-permute-done.13.r2 = bf16[37,64,256]{2,1,0:T(8,128)(2,1)} collective-permute-done((bf16[37,64,256]{2,1,0:T(8,128)(2,1)}, bf16[37,64,256]{2,1,0:T(8,128)(2,1)}, u32[]{:S(2)}, u32[]{:S(2)}) %collective-permute-start.13) | collective-permute-done | bytes 1212448 | tf_op jit(solution)/shard_map/ppermute | solution.py:299
  263.6 6.5 %pairs.1 = (f32[37,64,1024]{2,1,0:T(8,128)}, bf16[2,4,37,32,128]{4,3,2,1,0:T(8,128)(2,1)}) custom-call(s32[14]{0:T(128)} %get-tuple-element.23.info_ref.h_ref.where_ref, bf16[37,64,256]{2,1,0:T(8,128)(2,1)} %copy-done.7, bf16[37,64,256]{2,1,0:T(8,128)(2,1)} %copy-done.6, bf16[37,64,256]{2,1,0:T(8,128)(2,1)} %collective-permute-done.13.r2, ...), custom_call_target="tpu_custom_call" | custom-call | tf_op jit(solution)/shard_map/pairs/pallas_call | solution.py:359
  270.1 3.1 dynamic-slice_bitcast_fusion.8
  278.4 2.0 copy.60
  280.6 2.1 copy.59
  282.7 12.6 %rest.1 = (bf16[37,128,256]{2,1,0:T(8,128)(2,1)}, bf16[37,128,128]{2,1,0:T(8,128)(2,1)}) custom-call(s32[14]{0:T(128)} %get-tuple-element.23.info_ref.h_ref.where_ref, bf16[37,128,256]{2,1,0:T(8,128)(2,1)} %bitcast.92, bf16[37,128,256]{2,1,0:T(8,128)(2,1)} %bitcast.93, bf16[37,128,256]{2,1,0:T(8,128)(2,1)} %bitcast.94), custom_call_target="tpu_custom_call" | custom-call | flops 7274496 | bytes 7274496 | tf_op jit(solution)/shard_map/rest/pallas_call | solution.py:535
  295.3 2.0 constant_dynamic-slice_fusion
  298.3 11.9 %collective-permute-start.17 = (bf16[37,32,128]{2,1,0:T(8,128)(2,1)S(1)}, bf16[37,32,128]{2,1,0:T(8,128)(2,1)S(1)}, u32[]{:S(2)}, u32[]{:S(2)}) collective-permute-start(bf16[37,32,128]{2,1,0:T(8,128)(2,1)S(1)} %get-tuple-element.39), channel_id=1, source_target_pairs={{0,6},{1,7},{2,4},{3,5},{4,10},{5,11},{6,8},{7,9},{8,14},{9,15},{1... | collective-permute-start | bytes 909320 | tf_op jit(solution)/shard_map/ppermute | solution.py:574
  310.3 7.9 %collective-permute-start.16 = (bf16[37,32,128]{2,1,0:T(8,128)(2,1)S(1)}, bf16[37,32,128]{2,1,0:T(8,128)(2,1)S(1)}, u32[]{:S(2)}, u32[]{:S(2)}) collective-permute-start(bf16[37,32,128]{2,1,0:T(8,128)(2,1)S(1)} %get-tuple-element.40), channel_id=1, source_target_pairs={{0,5},{1,6},{2,7},{3,4},{4,9},{5,10},{6,11},{7,8},{8,13},{9,14},{1... | collective-permute-start | bytes 909320 | tf_op jit(solution)/shard_map/ppermute | solution.py:574
  319.2 1.9 collective-permute-done.18
  321.8 17.8 %collective-permute-done.17 = bf16[37,32,128]{2,1,0:T(8,128)(2,1)S(1)} collective-permute-done((bf16[37,32,128]{2,1,0:T(8,128)(2,1)S(1)}, bf16[37,32,128]{2,1,0:T(8,128)(2,1)S(1)}, u32[]{:S(2)}, u32[]{:S(2)}) %collective-permute-start.17) | collective-permute-done | bytes 303136 | tf_op jit(solution)/shard_map/ppermute | solution.py:574
  342.9 1.4 pad_maximum_fusion.1.far
  344.5 35.7 %collective-permute-done.7.e0 = bf16[37,64,128]{2,1,0:T(8,128)(2,1)S(1)} collective-permute-done((bf16[37,64,128]{2,1,0:T(8,128)(2,1)S(1)}, bf16[37,64,128]{2,1,0:T(8,128)(2,1)S(1)}, u32[]{:S(2)}, u32[]{:S(2)}) %collective-permute-start.7) | collective-permute-done | bytes 606240 | tf_op jit(solution)/shard_map/ppermute | solution.py:508
  380.2 13.0 %collective-permute-done.9.l0 = bf16[37,64,128]{2,1,0:T(8,128)(2,1)S(1)} collective-permute-done((bf16[37,64,128]{2,1,0:T(8,128)(2,1)S(1)}, bf16[37,64,128]{2,1,0:T(8,128)(2,1)S(1)}, u32[]{:S(2)}, u32[]{:S(2)}) %collective-permute-start.9) | collective-permute-done | bytes 606240 | tf_op jit(solution)/shard_map/ppermute | solution.py:508
  393.2 5.5 %place.1 = f32[37,64,1024]{2,1,0:T(8,128)} custom-call(s32[14]{0:T(128)S(1)} %copy-done, bf16[37,64,256]{2,1,0:T(8,128)(2,1)S(1)} %get-tuple-element.43.mine, bf16[37,64,256]{2,1,0:T(8,128)(2,1)S(1)} %collective-permute-done.6.other, bf16[37,64,128]{2,1,0:T(8,128)(2,1)S(1)} %collective-permute-done.7.e0, ...), custom_call_target="tpu_custom_call", output_to_operand_aliasing={{}: (9, {})} | custom-call | tf_op jit(solution)/shard_map/place/pallas_call | solution.py:475
  (75 shorter events, 19.6 us)
Async XLA Ops:
  6.9 20.5 %collective-permute-start = (bf16[64,24,256]{2,1,0:T(8,128)(2,1)}, bf16[64,24,256]{2,1,0:T(8,128)(2,1)S(1)}, u32[]{:S(2)}, u32[]{:S(2)}) collective-permute-start(bf16[64,24,256]{2,1,0:T(8,128)(2,1)} %get-tuple-element.59), channel_id=1, source_target_pairs={{0,1},{1,2},{2,3},{4,5},{5,6},{6,7},{8,9},{9,10},{10,11},{12,13},{... | collective-permute-start | bytes 2359304 | tf_op jit(solution)/shard_map/ppermute | solution.py:208
  10.1 12.8 %copy-start.13 = (f32[37]{0:T(128)S(1)}, f32[37]{0:T(128)}, u32[]{:S(2)}) copy-start(f32[37]{0:T(128)} %param.17) | copy-start | bytes 448
  12.5 14.9 %collective-permute-start.4 = (bf16[64,24,256]{2,1,0:T(8,128)(2,1)}, bf16[64,24,256]{2,1,0:T(8,128)(2,1)}, u32[]{:S(2)}, u32[]{:S(2)}) collective-permute-start(bf16[64,24,256]{2,1,0:T(8,128)(2,1)} %get-tuple-element.32), channel_id=1, source_target_pairs={{0,4},{4,8},{8,12},{1,5},{5,9},{9,13},{2,6},{6,10},{10,14},{3,7},{... | collective-permute-start | bytes 2359304 | tf_op jit(solution)/shard_map/ppermute | solution.py:208
  16.5 21.0 %collective-permute-start.1 = (bf16[64,24,256]{2,1,0:T(8,128)(2,1)S(1)}, bf16[64,24,256]{2,1,0:T(8,128)(2,1)S(1)}, u32[]{:S(2)}, u32[]{:S(2)}) collective-permute-start(bf16[64,24,256]{2,1,0:T(8,128)(2,1)S(1)} %get-tuple-element.58), channel_id=1, source_target_pairs={{1,0},{2,1},{3,2},{5,4},{6,5},{7,6},{9,8},{10,9},{11,10},{13,12},{... | collective-permute-start | bytes 2359304 | tf_op jit(solution)/shard_map/ppermute | solution.py:208
  18.5 18.9 %collective-permute-start.5 = (bf16[64,24,256]{2,1,0:T(8,128)(2,1)S(1)}, bf16[64,24,256]{2,1,0:T(8,128)(2,1)}, u32[]{:S(2)}, u32[]{:S(2)}) collective-permute-start(bf16[64,24,256]{2,1,0:T(8,128)(2,1)S(1)} %get-tuple-element.33), channel_id=1, source_target_pairs={{4,0},{8,4},{12,8},{5,1},{9,5},{13,9},{6,2},{10,6},{14,10},{7,3},{... | collective-permute-start | bytes 2359304 | tf_op jit(solution)/shard_map/ppermute | solution.py:208
  40.1 3.3 copy-start.10
  40.1 3.3 copy-start.11
  41.1 20.2 %collective-permute-start.3 = (bf16[64,48,24]{0,2,1:T(8,128)(2,1)S(1)}, bf16[64,48,24]{0,2,1:T(8,128)(2,1)S(1)}, u32[]{:S(2)}, u32[]{:S(2)}) collective-permute-start(bf16[64,48,24]{0,2,1:T(8,128)(2,1)S(1)} %copy.31), channel_id=1, source_target_pairs={{4,0},{8,4},{12,8},{5,1},{9,5},{13,9},{6,2},{10,6},{14,10},{7,3},{... | collective-permute-start | bytes 442376 | tf_op jit(solution)/shard_map/ppermute | solution.py:208
  45.6 11.6 %copy-start.12 = (s32[4]{0:T(128)S(1)}, s32[4]{0:T(128)}, u32[]{:S(2)}) copy-start(s32[4]{0:T(128)} %constant.79) | copy-start | bytes 52
  57.8 6.9 %collective-permute-start.2 = (bf16[64,48,24]{0,2,1:T(8,128)(2,1)S(1)}, bf16[64,48,24]{0,2,1:T(8,128)(2,1)S(1)}, u32[]{:S(2)}, u32[]{:S(2)}) collective-permute-start(bf16[64,48,24]{0,2,1:T(8,128)(2,1)S(1)} %copy.30), channel_id=1, source_target_pairs={{0,4},{4,8},{8,12},{1,5},{5,9},{9,13},{2,6},{6,10},{10,14},{3,7},{... | collective-permute-start | bytes 442376 | tf_op jit(solution)/shard_map/ppermute | solution.py:208
  70.6 1.1 copy-start.4
  70.6 1.4 copy-start.5
  159.6 80.2 %collective-permute-start.12 = (bf16[37,64,256]{2,1,0:T(8,128)(2,1)}, bf16[37,64,256]{2,1,0:T(8,128)(2,1)S(1)}, u32[]{:S(2)}, u32[]{:S(2)}) collective-permute-start(bf16[37,64,256]{2,1,0:T(8,128)(2,1)} %get-tuple-element.46), channel_id=1, source_target_pairs={{1,3},{4,2},{2,1},{8,0},{6,7},{9,6},{11,9},{14,8},{12,15},{3,13},{... | collective-permute-start | bytes 3637256 | tf_op jit(solution)/shard_map/ppermute | solution.py:299
  161.5 78.3 %collective-permute-start.11 = (bf16[37,64,256]{2,1,0:T(8,128)(2,1)}, bf16[37,64,256]{2,1,0:T(8,128)(2,1)S(1)}, u32[]{:S(2)}, u32[]{:S(2)}) collective-permute-start(bf16[37,64,256]{2,1,0:T(8,128)(2,1)} %get-tuple-element.47), channel_id=1, source_target_pairs={{1,2},{4,3},{2,0},{8,1},{6,6},{9,7},{11,8},{14,9},{12,14},{3,12},{... | collective-permute-start | bytes 3637256 | tf_op jit(solution)/shard_map/ppermute | solution.py:299
  230.2 20.4 %collective-permute-start.14 = (bf16[37,64,256]{2,1,0:T(8,128)(2,1)}, bf16[37,64,256]{2,1,0:T(8,128)(2,1)}, u32[]{:S(2)}, u32[]{:S(2)}) collective-permute-start(bf16[37,64,256]{2,1,0:T(8,128)(2,1)} %get-tuple-element.44), channel_id=1, source_target_pairs={{1,1},{4,0},{2,3},{8,2},{6,5},{9,4},{11,11},{14,10},{12,13},{3,15}... | collective-permute-start | bytes 3637256 | tf_op jit(solution)/shard_map/ppermute | solution.py:299
  232.5 31.1 %collective-permute-start.13 = (bf16[37,64,256]{2,1,0:T(8,128)(2,1)}, bf16[37,64,256]{2,1,0:T(8,128)(2,1)}, u32[]{:S(2)}, u32[]{:S(2)}) collective-permute-start(bf16[37,64,256]{2,1,0:T(8,128)(2,1)} %get-tuple-element.45), channel_id=1, source_target_pairs={{1,0},{4,1},{2,2},{8,3},{6,4},{9,5},{11,10},{14,11},{12,12},{3,14}... | collective-permute-start | bytes 3637256 | tf_op jit(solution)/shard_map/ppermute | solution.py:299
  239.8 23.8 %copy-start.6 = (bf16[37,64,256]{2,1,0:T(8,128)(2,1)}, bf16[37,64,256]{2,1,0:T(8,128)(2,1)S(1)}, u32[]{:S(2)}) copy-start(bf16[37,64,256]{2,1,0:T(8,128)(2,1)S(1)} %collective-permute-done.12.r1) | copy-start | bytes 3637252
  239.8 23.8 %copy-start.7 = (bf16[37,64,256]{2,1,0:T(8,128)(2,1)}, bf16[37,64,256]{2,1,0:T(8,128)(2,1)S(1)}, u32[]{:S(2)}) copy-start(bf16[37,64,256]{2,1,0:T(8,128)(2,1)S(1)} %collective-permute-done.11.r0) | copy-start | bytes 3637252
  270.1 8.3 %copy-start.1 = (bf16[128,37,256]{2,1,0:T(8,128)(2,1)S(1)}, bf16[128,37,256]{2,1,0:T(8,128)(2,1)}, u32[]{:S(2)}) copy-start(bf16[128,37,256]{2,1,0:T(8,128)(2,1)} %chain.2) | copy-start | bytes 7274500
  273.2 25.0 %collective-permute-start.19 = (bf16[37,32,128]{2,1,0:T(8,128)(2,1)}, bf16[37,32,128]{2,1,0:T(8,128)(2,1)}, u32[]{:S(2)}, u32[]{:S(2)}) collective-permute-start(bf16[37,32,128]{2,1,0:T(8,128)(2,1)} %get-tuple-element.34), channel_id=1, source_target_pairs={{0,8},{1,9},{2,10},{3,11},{12,4},{13,5},{14,6},{15,7},{16,24},{17,... | collective-permute-start | bytes 909320 | tf_op jit(solution)/shard_map/ppermute | solution.py:574
  274.5 23.8 %collective-permute-start.22 = (bf16[37,32,128]{2,1,0:T(8,128)(2,1)}, bf16[37,32,128]{2,1,0:T(8,128)(2,1)}, u32[]{:S(2)}, u32[]{:S(2)}) collective-permute-start(bf16[37,32,128]{2,1,0:T(8,128)(2,1)} %get-tuple-element.35), channel_id=1, source_target_pairs={{0,11},{1,8},{2,9},{3,10},{12,7},{13,4},{14,5},{15,6},{16,27},{17,... | collective-permute-start | bytes 909320 | tf_op jit(solution)/shard_map/ppermute | solution.py:574
  275.8 34.5 %collective-permute-start.21 = (bf16[37,32,128]{2,1,0:T(8,128)(2,1)}, bf16[37,32,128]{2,1,0:T(8,128)(2,1)}, u32[]{:S(2)}, u32[]{:S(2)}) collective-permute-start(bf16[37,32,128]{2,1,0:T(8,128)(2,1)} %get-tuple-element.36), channel_id=1, source_target_pairs={{0,10},{1,11},{2,8},{3,9},{12,6},{13,7},{14,4},{15,5},{16,26},{17,... | collective-permute-start | bytes 909320 | tf_op jit(solution)/shard_map/ppermute | solution.py:574
  277.1 41.0 %collective-permute-start.20 = (bf16[37,32,128]{2,1,0:T(8,128)(2,1)}, bf16[37,32,128]{2,1,0:T(8,128)(2,1)}, u32[]{:S(2)}, u32[]{:S(2)}) collective-permute-start(bf16[37,32,128]{2,1,0:T(8,128)(2,1)} %get-tuple-element.37), channel_id=1, source_target_pairs={{0,9},{1,10},{2,11},{3,8},{12,5},{13,6},{14,7},{15,4},{16,25},{17,... | collective-permute-start | bytes 909320 | tf_op jit(solution)/shard_map/ppermute | solution.py:574
  278.4 2.2 copy-start.2
  295.3 2.9 copy-start.9
  295.3 23.7 %copy-start.3 = (bf16[37,128,128]{2,1,0:T(8,128)(2,1)S(1)}, bf16[37,128,128]{2,1,0:T(8,128)(2,1)}, u32[]{:S(2)}) copy-start(bf16[37,128,128]{2,1,0:T(8,128)(2,1)} %own.1) | copy-start | bytes 3637252
  297.3 21.8 %copy-start.8 = (bf16[37,128,128]{2,1,0:T(8,128)(2,1)S(1)}, bf16[37,128,128]{2,1,0:T(8,128)(2,1)}, u32[]{:S(2)}) copy-start(bf16[37,128,128]{2,1,0:T(8,128)(2,1)} %get-tuple-element.27) | copy-start | bytes 3637252
  297.4 95.8 %collective-permute-start.6 = (bf16[37,64,256]{2,1,0:T(8,128)(2,1)S(1)}, bf16[37,64,256]{2,1,0:T(8,128)(2,1)S(1)}, u32[]{:S(2)}, u32[]{:S(2)}) collective-permute-start(bf16[37,64,256]{2,1,0:T(8,128)(2,1)S(1)} %get-tuple-element.42), channel_id=1, source_target_pairs={{0,1},{5,4},{10,11},{15,14},{16,17},{21,20},{26,27},{31,30}} | collective-permute-start | bytes 3637256 | tf_op jit(solution)/shard_map/ppermute | solution.py:566
  298.2 22.9 %collective-permute-start.18 = (bf16[37,32,128]{2,1,0:T(8,128)(2,1)S(1)}, bf16[37,32,128]{2,1,0:T(8,128)(2,1)S(1)}, u32[]{:S(2)}, u32[]{:S(2)}) collective-permute-start(bf16[37,32,128]{2,1,0:T(8,128)(2,1)S(1)} %copy-done.9), channel_id=1, source_target_pairs={{0,7},{1,4},{2,5},{3,6},{4,11},{5,8},{6,9},{7,10},{8,15},{9,12},{1... | collective-permute-start | bytes 909320 | tf_op jit(solution)/shard_map/ppermute | solution.py:574
  298.3 41.2 %collective-permute-start.17 = (bf16[37,32,128]{2,1,0:T(8,128)(2,1)S(1)}, bf16[37,32,128]{2,1,0:T(8,128)(2,1)S(1)}, u32[]{:S(2)}, u32[]{:S(2)}) collective-permute-start(bf16[37,32,128]{2,1,0:T(8,128)(2,1)S(1)} %get-tuple-element.39), channel_id=1, source_target_pairs={{0,6},{1,7},{2,4},{3,5},{4,10},{5,11},{6,8},{7,9},{8,14},{9,15},{1... | collective-permute-start | bytes 909320 | tf_op jit(solution)/shard_map/ppermute | solution.py:574
  310.3 30.6 %collective-permute-start.16 = (bf16[37,32,128]{2,1,0:T(8,128)(2,1)S(1)}, bf16[37,32,128]{2,1,0:T(8,128)(2,1)S(1)}, u32[]{:S(2)}, u32[]{:S(2)}) collective-permute-start(bf16[37,32,128]{2,1,0:T(8,128)(2,1)S(1)} %get-tuple-element.40), channel_id=1, source_target_pairs={{0,5},{1,6},{2,7},{3,4},{4,9},{5,10},{6,11},{7,8},{8,13},{9,14},{1... | collective-permute-start | bytes 909320 | tf_op jit(solution)/shard_map/ppermute | solution.py:574
  318.1 23.5 %collective-permute-start.15 = (bf16[37,32,128]{2,1,0:T(8,128)(2,1)S(1)}, bf16[37,32,128]{2,1,0:T(8,128)(2,1)S(1)}, u32[]{:S(2)}, u32[]{:S(2)}) collective-permute-start(bf16[37,32,128]{2,1,0:T(8,128)(2,1)S(1)} %get-tuple-element.41), channel_id=1, source_target_pairs={{0,4},{1,5},{2,6},{3,7},{4,8},{5,9},{6,10},{7,11},{8,12},{9,13},{1... | collective-permute-start | bytes 909320 | tf_op jit(solution)/shard_map/ppermute | solution.py:574
  321.1 23.4 %collective-permute-start.8 = (bf16[37,64,128]{2,1,0:T(8,128)(2,1)S(1)}, bf16[37,64,128]{2,1,0:T(8,128)(2,1)S(1)}, u32[]{:S(2)}, u32[]{:S(2)}) collective-permute-start(bf16[37,64,128]{2,1,0:T(8,128)(2,1)S(1)} %get-tuple-element.62), channel_id=1, source_target_pairs={{0,3},{5,7},{10,9},{15,13},{16,19},{21,23},{26,25},{31,29}} | collective-permute-start | bytes 1818632 | tf_op jit(solution)/shard_map/ppermute | solution.py:508
  339.6 40.6 %collective-permute-start.7 = (bf16[37,64,128]{2,1,0:T(8,128)(2,1)S(1)}, bf16[37,64,128]{2,1,0:T(8,128)(2,1)S(1)}, u32[]{:S(2)}, u32[]{:S(2)}) collective-permute-start(bf16[37,64,128]{2,1,0:T(8,128)(2,1)S(1)} %get-tuple-element.63), channel_id=1, source_target_pairs={{0,2},{5,6},{10,8},{15,12},{16,18},{21,22},{26,24},{31,28}} | collective-permute-start | bytes 1818632 | tf_op jit(solution)/shard_map/ppermute | solution.py:508
  340.9 39.3 %collective-permute-start.10 = (bf16[37,64,128]{2,1,0:T(8,128)(2,1)S(1)}, bf16[37,64,128]{2,1,0:T(8,128)(2,1)S(1)}, u32[]{:S(2)}, u32[]{:S(2)}) collective-permute-start(bf16[37,64,128]{2,1,0:T(8,128)(2,1)S(1)} %get-tuple-element.60), channel_id=1, source_target_pairs={{0,3},{5,7},{10,9},{15,13},{16,19},{21,23},{26,25},{31,29}} | collective-permute-start | bytes 1818632 | tf_op jit(solution)/shard_map/ppermute | solution.py:508
  341.6 51.6 %collective-permute-start.9 = (bf16[37,64,128]{2,1,0:T(8,128)(2,1)S(1)}, bf16[37,64,128]{2,1,0:T(8,128)(2,1)S(1)}, u32[]{:S(2)}, u32[]{:S(2)}) collective-permute-start(bf16[37,64,128]{2,1,0:T(8,128)(2,1)S(1)} %get-tuple-element.61), channel_id=1, source_target_pairs={{0,2},{5,6},{10,8},{15,12},{16,18},{21,22},{26,24},{31,28}} | collective-permute-start | bytes 1818632 | tf_op jit(solution)/shard_map/ppermute | solution.py:508
  344.3 48.9 %copy-start = (s32[14]{0:T(128)S(1)}, s32[14]{0:T(128)}, u32[]{:S(2)}) copy-start(s32[14]{0:T(128)} %get-tuple-element.23.info_ref.h_ref.where_ref) | copy-start | bytes 172
